TPU v7x, 32 devices: a whole 2x2x4 slice. The times are simulated.
32 devices in a mesh: groups: 2 (over x), right: 4 (over y, core), left: 4 (over z).
Axes of the slice: x: 2, y: 2, z: 4, core: 2. Of those that a mesh axis runs over, the one named last changes fastest.
Arguments:
- left_act: bfloat16 [4096, 8192], P(('groups', 'right'), 'left'), parts along dimension 0, may hold values from -15 to 15
- right_act: bfloat16 [4096, 4096], P(('groups', 'left'), 'right'), parts along dimension 0, may hold values from -15 to 15
- counts: int32 [512, 128], P(('groups', 'left'), 'right'), parts along dimension 0, may hold values from 512 to 2048
- w_out: bfloat16 [1024, 128], replicated, may hold values from -0.1875 to 0.1875
Outputs:
- pair_update: float32 [512, 128, 128], P(('groups', 'left'), 'right'), parts along dimension 0
There are 2 independent parts, one for each index of `groups`. A program takes and returns all parts, laid end to end along the dimension named above; an argument that names none is the same for every part. Nothing has to cross between parts.
All inputs are finite; a program needn't handle non-finite values.
Results may differ from a plain program's by a relative error of at most 0.0029.
Values may be sent and summed in bfloat16 or wider, within the bound.
A program may use at most 128 MiB of HBM per device.

v0:
```python
import functools

import jax
import jax.numpy as jnp
from jax import lax
from jax.experimental import pallas as pl
from jax.experimental.pallas import tpu as pltpu
from jax.sharding import PartitionSpec as P

CH = 32
CORES = 2
MESH = pl.DeviceIdType.MESH


def lane_quads(tiles):
    lane = lax.broadcasted_iota(jnp.int32, tiles[0].shape, 1)
    low = lane < 64
    even = (lane % 64) < 32
    stage = [None] * 4
    for c in range(2):
        a, b = tiles[c], tiles[c + 2]
        stage[c] = jnp.where(low, a, pltpu.roll(b, 64, 1))
        stage[c + 2] = jnp.where(low, pltpu.roll(a, 64, 1), b)
    outs = [None] * 4
    for half in range(2):
        a, b = stage[2 * half], stage[2 * half + 1]
        outs[2 * half] = jnp.where(even, a, pltpu.roll(b, 32, 1))
        outs[2 * half + 1] = jnp.where(even, pltpu.roll(a, 96, 1), b)
    return outs


def kernel(sizes, left_ref, right_ref, counts_ref, w_hbm, out_ref, w_ref, counts_in, cover, out_v, left_full, right_full, left_t, acc, flat,
           z_send, z_recv, y_send, y_recv, s_send, s_recv, own_sem, out_sem):
    n_z, n_r, q_z, q_y = sizes
    n_y = n_r // CORES
    rows_l, width_l = left_ref.shape
    rows_r, width_r = right_ref.shape
    piece_r = width_r // q_z
    piece_l = rows_l // q_y
    left_dev = width_l // CH
    right_dev = width_r // CH
    seqs = left_t.shape[1]
    z = lax.axis_index("left")
    r = lax.axis_index("right")
    y = r // CORES
    k = r % CORES

    def z_dev(pos):
        return {"left": pos}

    def y_dev(pos):
        return {"right": pos * CORES + k}

    sib_dev = {"right": y * CORES + (1 - k)}

    barrier = pltpu.get_barrier_semaphore()

    def greet(dev):
        pl.semaphore_signal(barrier, inc=1, device_id=dev, device_id_type=MESH)

    greet(sib_dev)
    for pos, n, dev in ((z, n_z, z_dev), (y, n_y, y_dev)):
        pl.when(pos + 1 < n)(functools.partial(greet, dev(pos + 1)))
        pl.when(pos >= 1)(functools.partial(greet, dev(pos - 1)))
    total = 1 + (z + 1 < n_z).astype(jnp.int32) + (z >= 1).astype(jnp.int32)
    total = total + (y + 1 < n_y).astype(jnp.int32) + (y >= 1).astype(jnp.int32)
    pl.semaphore_wait(barrier, total)

    def z_slot(chunk, q):
        return right_full.at[pl.ds(pl.multiple_of(chunk * rows_r, rows_r), rows_r), pl.ds(q * piece_r, piece_r)]

    def z_copy(side, step, q):
        sign = 1 - 2 * side
        chunk = z - sign * step
        src = right_ref.at[:, pl.ds(q * piece_r, piece_r)] if step == 0 else z_slot(chunk, q)
        at = step * q_z + q
        return pltpu.make_async_remote_copy(
            src_ref=src, dst_ref=z_slot(chunk, q), send_sem=z_send.at[side, at], recv_sem=z_recv.at[side, at],
            device_id=z_dev(z + sign), device_id_type=MESH)

    def z_sends(side, step):
        near = z + 1 < n_z if side == 0 else z >= 1
        far = z - step >= 0 if side == 0 else z + step < n_z
        return jnp.logical_and(near, far)

    def z_arrives(side, step):
        return z - step - 1 >= 0 if side == 0 else z + step + 1 < n_z

    def z_wait(side, step, q):
        sign = 1 - 2 * side
        slot = z_slot(z - sign * (step + 1), q)
        pltpu.make_async_copy(slot, slot, z_recv.at[side, step * q_z + q]).wait()

    def l_slot(chunk, q):
        return left_full.at[pl.ds(pl.multiple_of(chunk * rows_l + q * piece_l, piece_l), piece_l), :]

    def l_own(q):
        return left_ref.at[pl.ds(q * piece_l, piece_l), :]

    def y_copy(side, step, q):
        sign = 1 - 2 * side
        chunk = (y - sign * step) * CORES + k
        at = step * q_y + q
        return pltpu.make_async_remote_copy(
            src_ref=l_own(q) if step == 0 else l_slot(chunk, q), dst_ref=l_slot(chunk, q),
            send_sem=y_send.at[side, at], recv_sem=y_recv.at[side, at],
            device_id=y_dev(y + sign), device_id_type=MESH)

    def y_sends(side, step):
        near = y + 1 < n_y if side == 0 else y >= 1
        far = y - step >= 0 if side == 0 else y + step < n_y
        return jnp.logical_and(near, far)

    def y_arrives(side, step):
        return y - step - 1 >= 0 if side == 0 else y + step + 1 < n_y

    def y_wait(side, step, q):
        sign = 1 - 2 * side
        slot = l_slot((y - sign * (step + 1)) * CORES + k, q)
        pltpu.make_async_copy(slot, slot, y_recv.at[side, step * q_y + q]).wait()

    def s_at(side, step, q):
        if step < 0:
            return q
        return (1 + side * (n_y - 1) + step) * q_y + q

    def s_copy(side, step, q):
        sign = 1 - 2 * side
        chunk = (y - sign * (step + 1)) * CORES + k if step >= 0 else r
        at = s_at(side, step, q)
        return pltpu.make_async_remote_copy(
            src_ref=l_own(q) if step < 0 else l_slot(chunk, q), dst_ref=l_slot(chunk, q),
            send_sem=s_send.at[at], recv_sem=s_recv.at[at],
            device_id=sib_dev, device_id_type=MESH)

    def s_wait(side, step, q):
        sign = 1 - 2 * side
        y_from = y - sign * (step + 1) if step >= 0 else y
        slot = l_slot(y_from * CORES + (1 - k), q)
        pltpu.make_async_copy(slot, slot, s_recv.at[s_at(side, step, q)]).wait()

    tile = 256

    def turn(src, first_row, chunk, q):
        col = pl.multiple_of(chunk * rows_l + q * piece_l, piece_l)

        def body(m, carry):
            at = pl.multiple_of(m * tile, tile)
            left_t[pl.ds(at, tile), pl.ds(col, piece_l)] = src[pl.ds(first_row, piece_l), pl.ds(at, tile)].T
            return carry

        lax.fori_loop(0, width_l // tile, body, 0)

    def turn_full(chunk, q):
        turn(left_full, pl.multiple_of(chunk * rows_l + q * piece_l, piece_l), chunk, q)

    for q in range(max(q_z, q_y)):
        for side in range(2):
            if q < q_z:
                pl.when(z_sends(side, 0))(lambda side=side, q=q: z_copy(side, 0, q).start())
            if q < q_y:
                pl.when(y_sends(side, 0))(lambda side=side, q=q: y_copy(side, 0, q).start())
    own_left = pltpu.make_async_copy(left_ref, left_full.at[pl.ds(pl.multiple_of(r * rows_l, rows_l), rows_l), :], own_sem.at[0])
    own = pltpu.make_async_copy(right_ref, right_full.at[pl.ds(pl.multiple_of(z * rows_r, rows_r), rows_r), :], own_sem.at[1])
    weights = pltpu.make_async_copy(w_hbm, w_ref, own_sem.at[2])
    counts_copy = pltpu.make_async_copy(counts_ref, counts_in, own_sem.at[3])
    for copy in (own_left, own, weights, counts_copy):
        copy.start()
    for q in range(q_y):
        s_copy(0, -1, q).start()
    own_left.wait()
    for q in range(q_y):
        turn_full(r, q)
    counts_copy.wait()
    counted = counts_in[...].astype(jnp.float32)
    for j in range(right_dev):
        cover[j] = jnp.broadcast_to(counted[:, j:j + 1], (left_dev, cover.shape[2]))
    for q in range(q_y):
        s_wait(0, -1, q)
        turn_full(y * CORES + (1 - k), q)

    def z_tick(step, q):
        for side in range(2):
            @pl.when(z_arrives(side, step))
            def _():
                z_wait(side, step, q)
                if step + 1 < n_z - 1:
                    pl.when(z_sends(side, step + 1))(lambda: z_copy(side, step + 1, q).start())

    def y_tick(step, q):
        for side in range(2):
            @pl.when(y_arrives(side, step))
            def _():
                y_wait(side, step, q)
                s_copy(side, step, q).start()
                if step + 1 < n_y - 1:
                    pl.when(y_sends(side, step + 1))(lambda: y_copy(side, step + 1, q).start())

        for side in range(2):
            @pl.when(y_arrives(side, step))
            def _():
                sign = 1 - 2 * side
                y_from = y - sign * (step + 1)
                turn_full(y_from * CORES + k, q)
                s_wait(side, step, q)
                turn_full(y_from * CORES + (1 - k), q)

    y_ticks = [(step, q) for step in range(n_y - 1) for q in range(q_y)]
    for t in range((n_z - 2) * q_z):
        z_tick(t // q_z, t % q_z)
        if t % 2 == 1 and y_ticks:
            y_tick(*y_ticks.pop(0))
    for tick in y_ticks:
        y_tick(*tick)
    own.wait()
    weights.wait()

    block = 1024
    at_end = jnp.logical_or(z == 0, z == n_z - 1)
    base = jnp.where(z == 0, 0, rows_r)
    base = pl.multiple_of(base, rows_r)

    def product(q, first, depth, add):
        cols = pl.ds(q * piece_r, piece_r)

        def body(m, carry):
            rows = pl.ds(pl.multiple_of(m * block, block), block)
            value = jnp.dot(left_t[rows, pl.ds(first, depth)], right_full[pl.ds(first, depth), cols],
                            preferred_element_type=jnp.float32)
            for part in range(piece_r // 128):
                some = value[:, part * 128:(part + 1) * 128]
                slab = q * (piece_r // 128) + part
                acc[slab, rows, :] = acc[slab, rows, :] + some if add else some
            return carry

        lax.fori_loop(0, width_l // block, body, 0)

    def first_part(q):
        @pl.when(at_end)
        def _():
            product(q, base, seqs - rows_r, False)

        @pl.when(jnp.logical_not(at_end))
        def _():
            product(q, 0, seqs, False)

    for q in range(q_z):
        first_part(q)

    def finish(q):
        heads = piece_r // CH
        for quad in range(heads // 4):
            slab = acc.at[q * (piece_r // 128) + quad]
            for cq in range(CH // 4):
                tiles = [slab[pl.ds(cq * 4 + c, left_dev, stride=CH), :].astype(jnp.bfloat16) for c in range(4)]
                for j, value in enumerate(lane_quads(tiles)):
                    flat[pl.ds((quad * 4 + j) * left_dev, left_dev), pl.ds(cq * 128, 128)] = value
        projected = jnp.dot(flat[...], w_ref[...], preferred_element_type=jnp.float32)
        for j in range(heads):
            value = projected[j * left_dev:(j + 1) * left_dev, :] / cover[q * heads + j]
            out_v.at[q].reshape(left_dev * heads, value.shape[1])[pl.ds(j, left_dev, stride=heads), :] = value
        out_copy(q).start()

    def out_copy(q):
        return pltpu.make_async_copy(out_v.at[q], out_ref.at[:, pl.ds(q * heads_q, heads_q), :], out_sem.at[q])

    heads_q = piece_r // CH
    last = n_z - 2
    for q in range(q_z):
        z_tick(last, q)

        @pl.when(at_end)
        def _():
            far = jnp.where(z == 0, (n_z - 1) * rows_r, 0)
            product(q, pl.multiple_of(far, rows_r), rows_r, True)

        finish(q)

    for side in range(2):
        for step in range(n_z - 1):
            for q in range(q_z):
                pl.when(z_sends(side, step))(lambda side=side, step=step, q=q: z_copy(side, step, q).wait_send())
        for step in range(n_y - 1):
            for q in range(q_y):
                pl.when(y_sends(side, step))(lambda side=side, step=step, q=q: y_copy(side, step, q).wait_send())
                pl.when(y_arrives(side, step))(lambda side=side, step=step, q=q: s_copy(side, step, q).wait_send())
    for q in range(q_y):
        s_copy(0, -1, q).wait_send()
    for q in range(q_z):
        out_copy(q).wait()


def solution(mesh):
    n_z, n_r = mesh.shape["left"], mesh.shape["right"]
    n_y = n_r // CORES

    def shards(left_act, right_act, counts, w_out):
        rows_l, width_l = left_act.shape
        rows_r, width_r = right_act.shape
        seqs = rows_r * n_z
        left_dev, right_dev = counts.shape
        pair = w_out.shape[1]
        q_z = width_r // 256
        q_y = rows_l // max(128, rows_l // 4)
        projected = pl.pallas_call(
            functools.partial(kernel, (n_z, n_r, q_z, q_y)),
            out_shape=jax.ShapeDtypeStruct((left_dev, right_dev, pair), jnp.float32),
            in_specs=[pl.BlockSpec(memory_space=pl.ANY)] * 4,
            out_specs=pl.BlockSpec(memory_space=pl.ANY),
            scratch_shapes=[
                pltpu.VMEM(w_out.shape, w_out.dtype),
                pltpu.VMEM(counts.shape, counts.dtype),
                pltpu.VMEM((right_dev, left_dev, pair), jnp.float32),
                pltpu.VMEM((q_z, left_dev, right_dev // q_z, pair), jnp.float32),
                pltpu.VMEM((seqs, width_l), jnp.bfloat16),
                pltpu.VMEM((seqs, width_r), jnp.bfloat16),
                pltpu.VMEM((width_l, seqs), jnp.bfloat16),
                pltpu.VMEM((width_r // 128, width_l, 128), jnp.float32),
                pltpu.VMEM((width_r // q_z // CH * left_dev, CH * CH), jnp.bfloat16),
                pltpu.SemaphoreType.DMA((2, (n_z - 1) * q_z)),
                pltpu.SemaphoreType.DMA((2, (n_z - 1) * q_z)),
                pltpu.SemaphoreType.DMA((2, (n_y - 1) * q_y)),
                pltpu.SemaphoreType.DMA((2, (n_y - 1) * q_y)),
                pltpu.SemaphoreType.DMA(((2 * n_y - 1) * q_y,)),
                pltpu.SemaphoreType.DMA(((2 * n_y - 1) * q_y,)),
                pltpu.SemaphoreType.DMA((4,)),
                pltpu.SemaphoreType.DMA((q_z,)),
            ],
            compiler_params=pltpu.CompilerParams(
                collective_id=0, has_side_effects=True, vmem_limit_bytes=56 * 1024 * 1024
            ),
            name="pair_mean",
        )(left_act, right_act, counts, w_out)
        return projected

    in_specs = (
        P(("groups", "right"), "left"),
        P(("groups", "left"), "right"),
        P(("groups", "left"), "right"),
        P(),
    )
    out_specs = P(("groups", "left"), "right", None)
    return jax.shard_map(shards, mesh=mesh, in_specs=in_specs, out_specs=out_specs, check_vma=False)
```

profile of v0, /device:TPU:0, one launch (start us, length us, event | category | flops | bytes accessed | tf_op | source)
XLA Modules:
  0.0 80.5 jit_solution(15863092043330643589)
XLA Ops:
  0.0 1.4 %copy.5.counts_ref = s32[64,32]{1,0:T(8,128)} copy(s32[64,32]{0,1:T(8,128)} %param.6) | data formatting | bytes 16384 | tf_op args[2]
  1.4 76.8 %pair_mean.1 = f32[64,32,128]{2,1,0:T(8,128)} custom-call(bf16[512,2048]{1,0:T(8,128)(2,1)} %left_ref.1, bf16[512,1024]{1,0:T(8,128)(2,1)} %right_ref.1, s32[64,32]{1,0:T(8,128)} %copy.5.counts_ref, bf16[1024,128]{1,0:T(8,128)(2,1)} %w_hbm.1), custom_call_target="tpu_custom_call" | custom-call | tf_op jit(solution)/shard_map/pair_mean/pallas_call | solution.py:305
  78.2 2.3 %copy.7 = f32[64,32,128]{2,1,0:T(8,128)} copy(f32[64,32,128]{2,1,0:T(8,128)} %pair_mean.1) | data formatting | bytes 2097152
where the time goes:
time: 80.7 us; the launch traced here: 80.5 us
  Pallas kernels  76.8 us (95%)
  local copies, waits for them, and re-layouts  3.68 us (5%)
    pallas_call x1, Pallas kernels, shards(): pl.pallas_call(functools.partial(kernel, (n_z, n_r, q_z, q_y)), out_shape...  76.8 us
    unnamed x2, local copies, waits for them, and re-layouts  3.68 us

commit v1 on v0

--- a/solution.py
+++ b/solution.py
@@ -9,6 +9,7 @@
 
 CH = 32
 CORES = 2
+TILE = 256
 MESH = pl.DeviceIdType.MESH
 
 
@@ -290,11 +291,358 @@
         out_copy(q).wait()
 
 
+def folded(left_ref, right_ref, counts_ref, w_hbm, out_ref, w_in, w_wide, w_ref, counts_in, cover, order, left_full, left_far, right_full, right_t,
+           acc, acc_far, flat, part, out_v, in_send, in_recv, fwd_send, far_send, far_recv, end_send, end_recv, own_send, own_recv,
+           y_send, y_recv, s_send, s_recv, a_send, a_recv, p_send, p_recv, own_sem, out_sem):
+    rows, width_l = left_ref.shape
+    width_r = right_ref.shape[1]
+    steps = width_r // TILE
+    piece = rows // steps
+    half = width_l // CORES
+    quads = width_l // 128
+    heads = TILE // CH
+    z = lax.axis_index("left")
+    r = lax.axis_index("right")
+    y, k = r // CORES, r % CORES
+    up = z // 2
+    sign = 2 * up - 1
+
+    def fold(n, at):
+        return up * at + (1 - up) * (n - 1 - at)
+
+    zc, yc, kc = fold(4, z), fold(2, y), fold(2, k)
+    inner, end = zc == 2, zc == 3
+    sib_dev = {"right": r + 1 - 2 * k}
+    y_dev = {"right": r + (1 - 2 * y) * CORES}
+
+    def when(*terms):
+        value = terms[0]
+        for term in terms[1:]:
+            value = jnp.logical_and(value, term)
+        return pl.when(value)
+
+    def z_dev(way):
+        return {"left": z + way * sign}
+
+    barrier = pltpu.get_barrier_semaphore()
+
+    def greet(dev):
+        pl.semaphore_signal(barrier, inc=1, device_id=dev, device_id_type=MESH)
+
+    greet(sib_dev)
+    greet(y_dev)
+    greet(z_dev(-1))
+    when(inner)(lambda: greet(z_dev(1)))
+    pl.semaphore_wait(barrier, 3 + inner.astype(jnp.int32))
+
+    def remote(src, dst, send, recv, dev):
+        return pltpu.make_async_remote_copy(src_ref=src, dst_ref=dst, send_sem=send, recv_sem=recv, device_id=dev, device_id_type=MESH)
+
+    def arrived(slot, sem):
+        pltpu.make_async_copy(slot, slot, sem).wait()
+
+    def block(at, first=0, size=rows):
+        return pl.ds(pl.multiple_of(fold(4, at) * rows + first, size), size)
+
+    def cols(q):
+        return pl.ds(pl.multiple_of(q * TILE, TILE), TILE)
+
+    def right_slot(at, q):
+        return right_full.at[block(at), cols(q)]
+
+    def in_copy(way, q):
+        return remote(right_ref.at[:, cols(q)], right_slot(2, q), in_send.at[(way + 1) // 2, q], in_recv.at[0, q], z_dev(way))
+
+    def fwd_copy(way, q):
+        slot = right_slot(3 if way < 0 else 1, q)
+        return remote(slot, slot, fwd_send.at[(way + 1) // 2, q], in_recv.at[1, q], z_dev(way))
+
+    def end_copy(q):
+        return remote(right_ref.at[:, cols(q)], right_slot(3, q), end_send.at[q], end_recv.at[q], z_dev(-1))
+
+    def own_half():
+        return pl.ds(pl.multiple_of(k * half, half), half)
+
+    def far_copy(p):
+        at = pl.ds(pl.multiple_of(p * piece, piece), piece)
+        return remote(left_full.at[block(0, p * piece, piece), own_half()], left_far.at[at, own_half()], far_send.at[p], far_recv.at[p], z_dev(-1))
+
+    def far_slot(p, core):
+        return left_far.at[pl.ds(pl.multiple_of(p * piece, piece), piece), pl.ds(pl.multiple_of(core * half, half), half)]
+
+    def share_copy(p):
+        return remote(far_slot(p, k), far_slot(p, k), a_send.at[p], a_recv.at[p], sib_dev)
+
+    def own_copy(p):
+        at = pl.ds(pl.multiple_of(p * piece, piece), piece)
+        slot = left_full.at[pl.ds(pl.multiple_of(r * rows + p * piece, piece), piece), :]
+        return remote(left_ref.at[at, :], slot, own_send.at[p], own_recv.at[p], sib_dev)
+
+    def own_arrived(p):
+        other = r + 1 - 2 * k
+        arrived(left_full.at[pl.ds(pl.multiple_of(other * rows + p * piece, piece), piece), :], own_recv.at[p])
+
+    def y_slot(side, pos, p, core):
+        return left_full.at[block(2 * side + pos, p * piece, piece), pl.ds(pl.multiple_of(core * half, half), half)]
+
+    def y_copy(pos, p):
+        slot = y_slot(yc, pos, p, k)
+        return remote(slot, slot, y_send.at[pos, p], y_recv.at[pos, p], y_dev)
+
+    def s_copy(pos, p):
+        slot = y_slot(1 - yc, pos, p, k)
+        return remote(slot, slot, s_send.at[pos, p], s_recv.at[pos, p], sib_dev)
+
+    def part_copy(q):
+        return remote(part.at[q], part.at[q], p_send.at[q], p_recv.at[q], z_dev(1))
+
+    def each(body, first=0, last=steps):
+        def step(at, carry):
+            body(at)
+            return carry
+
+        lax.fori_loop(first, last, step, 0)
+
+    @when(inner)
+    def _():
+        @each
+        def _(q):
+            in_copy(-1, q).start()
+            in_copy(1, q).start()
+
+    when(end)(lambda: end_copy(0).start())
+    own_left = pltpu.make_async_copy(left_ref, left_full.at[pl.ds(pl.multiple_of(r * rows, rows), rows), :], own_sem.at[0])
+    own = pltpu.make_async_copy(right_ref, right_full.at[block(zc), :], own_sem.at[1])
+    weights = pltpu.make_async_copy(w_hbm, w_in, own_sem.at[2])
+    counts_copy = pltpu.make_async_copy(counts_ref, counts_in, own_sem.at[3])
+    own_left.start()
+    each(lambda p: own_copy(p).start())
+    for copy in (own, weights, counts_copy):
+        copy.start()
+    own_left.wait()
+    first, second = kc == 0, kc == 1
+
+    @when(first)
+    def _():
+        each(lambda p: y_copy(0, p).start())
+        when(end, yc == 0)(lambda: each(lambda p: far_copy(p).start()))
+
+    @each
+    def _(p):
+        own_arrived(p)
+
+        @when(second)
+        def _():
+            y_copy(0, p).start()
+            when(end, yc == 0)(lambda: far_copy(p).start())
+
+    each(lambda p: y_copy(1, p).start())
+    when(end, yc == 0)(lambda: each(lambda q: end_copy(q).start(), 1))
+
+    row = lax.broadcasted_iota(jnp.int32, (TILE, TILE), 0)
+    column = lax.broadcasted_iota(jnp.int32, (TILE, TILE), 1)
+    order[...] = jnp.where(column == (row % heads) * CH + row // heads, 1.0, 0.0).astype(order.dtype)
+    weights.wait()
+    w_wide[...] = w_in[...].astype(jnp.float32)
+    for e in range(CH):
+        w_ref[pl.ds(e * CH, CH), :] = w_wide[pl.ds(e, CH, stride=CH), :].astype(w_ref.dtype)
+    counts_copy.wait()
+    counted = counts_in[...].astype(jnp.float32)
+    for i in range(counted.shape[1]):
+        cover[i // 4, i % 4] = jnp.broadcast_to(counted[:, i:i + 1], (counted.shape[0], cover.shape[3]))
+
+    def turn(at, q):
+        value = lax.dot_general(order[...], right_full[block(at), cols(q)], (((1,), (1,)), ((), ())), preferred_element_type=jnp.float32)
+        right_t[cols(q), block(at)] = value.astype(right_t.dtype)
+
+    def product(into, lines, source, left, left_rows, size, add):
+        wide = 512
+        lhs = right_t.at[lines, source]
+
+        @functools.partial(each, last=width_l // wide)
+        def _(n):
+            value = jnp.dot(lhs[...], left[left_rows, pl.ds(pl.multiple_of(n * wide, wide), wide)], preferred_element_type=jnp.float32)
+            for one in range(wide // 128):
+                some = value[:, one * 128:(one + 1) * 128]
+                slab = n * (wide // 128) + one
+                into[slab, size, :] = into[slab, size, :] + some if add else some
+
+    def product_all(at, add):
+        every = pl.ds(0, width_r)
+        product(acc, every, block(at), left_full, block(at), every, add)
+
+    def product_one(at, q):
+        product(acc, cols(q), block(at), left_full, block(at), cols(q), True)
+
+    def project(source, first_row):
+        for eq in range(CH // 4):
+            tiles = []
+            for e in range(4):
+                tile = source[:, pl.ds(pl.multiple_of(first_row + (eq * 4 + e) * heads, heads), heads), :]
+                tiles.append(tile.reshape(quads * heads, 128).astype(flat.dtype))
+            for i, value in enumerate(lane_quads(tiles)):
+                flat[pl.ds(i * quads * heads, quads * heads), pl.ds(eq * 128, 128)] = value
+        return jnp.dot(flat[...], w_ref[...], preferred_element_type=jnp.float32)
+
+    def settle(q, add):
+        for i in range(4):
+            value = out_v[q, :, i]
+            if add:
+                more = part[q, pl.ds(i * quads * heads, quads * heads), :]
+                value = value + more.astype(jnp.float32).reshape(value.shape)
+            out_v[q, :, i] = value / cover[:, i, pl.ds(pl.multiple_of(q * heads, heads), heads), :]
+        out_copy(q).start()
+
+    def out_copy(q):
+        at = pl.ds(pl.multiple_of(q * heads, heads), heads)
+        return pltpu.make_async_copy(out_v.at[q].reshape(4 * quads, heads, 128), out_ref.at[:, at, :], out_sem.at[q])
+
+    own.wait()
+    each(lambda q: turn(zc, q))
+
+    @each
+    def _(p):
+        arrived(right_slot(zc - 1, p), in_recv.at[0, p])
+        when(inner)(lambda: fwd_copy(1, p).start())
+        arrived(y_slot(1 - yc, 0, p, k), y_recv.at[0, p])
+        s_copy(0, p).start()
+        when(end, yc == 1)(lambda: far_copy(p).start())
+
+        @when(inner, p >= 1)
+        def _():
+            arrived(far_slot(p - 1, k), far_recv.at[p - 1])
+            share_copy(p - 1).start()
+
+        turn(zc - 1, p)
+
+    when(end, yc == 1)(lambda: each(lambda q: end_copy(q).start(), 1))
+
+    def end_arrived(q):
+        arrived(right_slot(3, q), end_recv.at[q])
+        fwd_copy(-1, q).start()
+        turn(3, q)
+
+    when(inner)(lambda: end_arrived(0))
+    each(lambda p: arrived(y_slot(1 - yc, 0, p, 1 - k), s_recv.at[0, p]))
+    product_all(2, False)
+    near, late = 1 + 2 * yc, 3 - 2 * yc
+
+    def far(q):
+        arrived(right_slot(0, q), in_recv.at[1, q])
+        turn(0, q)
+        product(acc_far, cols(q), block(0), left_far, pl.ds(0, rows), pl.ds(0, TILE), False)
+        part[q] = project(acc_far, 0).astype(part.dtype)
+        product_one(0, q)
+        part_copy(q).start()
+
+    @each
+    def _(q):
+        when(inner, q >= 1)(lambda: end_arrived(q))
+        arrived(y_slot(1 - yc, 1, q, k), y_recv.at[1, q])
+        s_copy(1, q).start()
+
+        @when(end)
+        def _():
+            arrived(right_slot(1, q), in_recv.at[1, q])
+            turn(1, q)
+
+        product_one(near, q)
+
+        @when(inner, q == 0)
+        def _():
+            arrived(far_slot(steps - 1, k), far_recv.at[steps - 1])
+            share_copy(steps - 1).start()
+            each(lambda p: arrived(far_slot(p, 1 - k), a_recv.at[p]))
+
+        when(inner, q >= 1)(lambda: far(q - 1))
+
+    each(lambda p: arrived(y_slot(1 - yc, 1, p, 1 - k), s_recv.at[1, p]))
+    product_all(late, True)
+
+    @each
+    def _(q):
+        when(inner, q == steps - 1)(lambda: far(q))
+        value = project(acc, q * TILE)
+        for i in range(4):
+            out_v[q, :, i] = value[i * quads * heads:(i + 1) * quads * heads].reshape(quads, heads, 128)
+        when(inner)(lambda: settle(q, False))
+
+    @when(end)
+    def _():
+        @each
+        def _(q):
+            arrived(part.at[q], p_recv.at[q])
+            settle(q, True)
+
+    @each
+    def _(q):
+        own_copy(q).wait_send()
+        for pos in range(2):
+            y_copy(pos, q).wait_send()
+            s_copy(pos, q).wait_send()
+
+        @when(inner)
+        def _():
+            for way in (-1, 1):
+                in_copy(way, q).wait_send()
+                fwd_copy(way, q).wait_send()
+            share_copy(q).wait_send()
+            part_copy(q).wait_send()
+
+        @when(end)
+        def _():
+            end_copy(q).wait_send()
+            far_copy(q).wait_send()
+
+        out_copy(q).wait()
+
+
+def folded_call(left_act, right_act, counts, w_out):
+    rows, width_l = left_act.shape
+    width_r = right_act.shape[1]
+    left_dev, right_dev = counts.shape
+    pair = w_out.shape[1]
+    steps = width_r // TILE
+    heads = TILE // CH
+    full = 4 * rows
+    dma = pltpu.SemaphoreType.DMA
+    return pl.pallas_call(
+        folded,
+        out_shape=jax.ShapeDtypeStruct((left_dev, right_dev, pair), jnp.float32),
+        in_specs=[pl.BlockSpec(memory_space=pl.ANY)] * 4,
+        out_specs=pl.BlockSpec(memory_space=pl.ANY),
+        scratch_shapes=[
+            pltpu.VMEM(w_out.shape, w_out.dtype),
+            pltpu.VMEM(w_out.shape, jnp.float32),
+            pltpu.VMEM(w_out.shape, w_out.dtype),
+            pltpu.VMEM((right_dev, left_dev), counts.dtype),
+            pltpu.VMEM((left_dev // 4, 4, right_dev, pair), jnp.float32),
+            pltpu.VMEM((TILE, TILE), jnp.bfloat16),
+            pltpu.VMEM((full, width_l), jnp.bfloat16),
+            pltpu.VMEM((rows, width_l), jnp.bfloat16),
+            pltpu.VMEM((full, width_r), jnp.bfloat16),
+            pltpu.VMEM((width_r, full), jnp.bfloat16),
+            pltpu.VMEM((width_l // 128, width_r, 128), jnp.float32),
+            pltpu.VMEM((width_l // 128, TILE, 128), jnp.float32),
+            pltpu.VMEM((left_dev * heads, CH * CH), jnp.bfloat16),
+            pltpu.VMEM((steps, left_dev * heads, pair), jnp.bfloat16),
+            pltpu.VMEM((steps, left_dev // 4, 4, heads, pair), jnp.float32),
+            dma((2, steps)), dma((2, steps)), dma((2, steps)), dma((steps,)), dma((steps,)), dma((steps,)), dma((steps,)), dma((steps,)),
+            dma((steps,)), dma((2, steps)), dma((2, steps)), dma((2, steps)), dma((2, steps)), dma((steps,)), dma((steps,)), dma((steps,)),
+            dma((steps,)), dma((4,)), dma((steps,)),
+        ],
+        compiler_params=pltpu.CompilerParams(collective_id=0, has_side_effects=True, vmem_limit_bytes=56 * 1024 * 1024),
+        name="pair_mean",
+    )(left_act, right_act, counts.T, w_out)
+
+
 def solution(mesh):
     n_z, n_r = mesh.shape["left"], mesh.shape["right"]
     n_y = n_r // CORES
 
     def shards(left_act, right_act, counts, w_out):
+        if (n_z, n_y) == (4, 2):
+            return folded_call(left_act, right_act, counts, w_out)
         rows_l, width_l = left_act.shape
         rows_r, width_r = right_act.shape
         seqs = rows_r * n_z

time: 80.7 us -> 77.9 us (0.965)
  local copies, waits for them, and re-layouts: 3.68 us -> 2.26 us
  Pallas kernels: 76.8 us -> 75.4 us
    unnamed x2 -> x1, local copies, waits for them, and re-layouts: 3.68 us -> 2.26 us
    pallas_call x1, Pallas kernels: 76.8 us -> 75.4 us  [folded_call(): pl.pallas_call(folded, out_shape=jax.ShapeDtypeStruct((left_dev, right_de...]
where the time goes in v1:
time: 77.9 us; the launch traced here: 77.7 us
  Pallas kernels  75.4 us (97%)
  local copies, waits for them, and re-layouts  2.26 us (3%)
    pallas_call x1, Pallas kernels, folded_call(): pl.pallas_call(folded, out_shape=jax.ShapeDtypeStruct((left_dev, right_de...  75.4 us
    unnamed x1, local copies, waits for them, and re-layouts  2.26 us

profile of v1, /device:TPU:0, one launch (start us, length us, event | category | flops | bytes accessed | tf_op | source)
XLA Modules:
  0.0 77.7 jit_solution(10457302349265109540)
XLA Ops:
  0.0 75.4 %pair_mean.1 = f32[64,32,128]{2,1,0:T(8,128)} custom-call(bf16[512,2048]{1,0:T(8,128)(2,1)} %left_ref.1, bf16[512,1024]{1,0:T(8,128)(2,1)} %right_ref.1, s32[32,64]{1,0:T(8,128)} %bitcast.1, bf16[1024,128]{1,0:T(8,128)(2,1)} %w_hbm.1), custom_call_target="tpu_custom_call" | custom-call | tf_op jit(solution)/shard_map/pair_mean/pallas_call | solution.py:609
  75.5 2.3 %copy.6 = f32[64,32,128]{2,1,0:T(8,128)} copy(f32[64,32,128]{2,1,0:T(8,128)} %pair_mean.1) | data formatting | bytes 2097152

commit v2 on v1

--- a/solution.py
+++ b/solution.py
@@ -301,6 +301,7 @@
     half = width_l // CORES
     quads = width_l // 128
     heads = TILE // CH
+    early = steps // 2
     z = lax.axis_index("left")
     r = lax.axis_index("right")
     y, k = r // CORES, r % CORES
@@ -383,11 +384,13 @@
         arrived(left_full.at[pl.ds(pl.multiple_of(other * rows + p * piece, piece), piece), :], own_recv.at[p])
 
     def y_slot(side, pos, p, core):
-        return left_full.at[block(2 * side + pos, p * piece, piece), pl.ds(pl.multiple_of(core * half, half), half)]
-
-    def y_copy(pos, p):
+        at = 3 * side if pos == 0 else 1 + side
+        return left_full.at[block(at, p * piece, piece), pl.ds(pl.multiple_of(core * half, half), half)]
+
+    def y_copy(pos, p, own=False):
         slot = y_slot(yc, pos, p, k)
-        return remote(slot, slot, y_send.at[pos, p], y_recv.at[pos, p], y_dev)
+        source = left_ref.at[pl.ds(pl.multiple_of(p * piece, piece), piece), own_half()] if own else slot
+        return remote(source, slot, y_send.at[pos, p], y_recv.at[pos, p], y_dev)
 
     def s_copy(pos, p):
         slot = y_slot(1 - yc, pos, p, k)
@@ -402,6 +405,9 @@
             return carry
 
         lax.fori_loop(first, last, step, 0)
+
+    first = kc == yc
+    when(first)(lambda: each(lambda p: y_copy(0, p, True).start()))
 
     @when(inner)
     def _():
@@ -410,34 +416,25 @@
             in_copy(-1, q).start()
             in_copy(1, q).start()
 
-    when(end)(lambda: end_copy(0).start())
+    when(end)(lambda: each(lambda q: end_copy(q).start(), 0, early))
     own_left = pltpu.make_async_copy(left_ref, left_full.at[pl.ds(pl.multiple_of(r * rows, rows), rows), :], own_sem.at[0])
     own = pltpu.make_async_copy(right_ref, right_full.at[block(zc), :], own_sem.at[1])
     weights = pltpu.make_async_copy(w_hbm, w_in, own_sem.at[2])
     counts_copy = pltpu.make_async_copy(counts_ref, counts_in, own_sem.at[3])
-    own_left.start()
     each(lambda p: own_copy(p).start())
-    for copy in (own, weights, counts_copy):
+    for copy in (own_left, own, weights, counts_copy):
         copy.start()
-    own_left.wait()
-    first, second = kc == 0, kc == 1
-
-    @when(first)
-    def _():
-        each(lambda p: y_copy(0, p).start())
-        when(end, yc == 0)(lambda: each(lambda p: far_copy(p).start()))
 
     @each
     def _(p):
         own_arrived(p)
-
-        @when(second)
-        def _():
-            y_copy(0, p).start()
-            when(end, yc == 0)(lambda: far_copy(p).start())
-
+        when(jnp.logical_not(first))(lambda: y_copy(0, p).start())
+        when(end, yc == 0, kc == 1)(lambda: far_copy(p).start())
+
+    own_left.wait()
+    when(end, yc == 0, kc == 0)(lambda: each(lambda p: far_copy(p).start()))
     each(lambda p: y_copy(1, p).start())
-    when(end, yc == 0)(lambda: each(lambda q: end_copy(q).start(), 1))
+    when(end, yc == 0)(lambda: each(lambda q: end_copy(q).start(), early))
 
     row = lax.broadcasted_iota(jnp.int32, (TILE, TILE), 0)
     column = lax.broadcasted_iota(jnp.int32, (TILE, TILE), 1)
@@ -455,24 +452,20 @@
         value = lax.dot_general(order[...], right_full[block(at), cols(q)], (((1,), (1,)), ((), ())), preferred_element_type=jnp.float32)
         right_t[cols(q), block(at)] = value.astype(right_t.dtype)
 
-    def product(into, lines, source, left, left_rows, size, add):
-        wide = 512
-        lhs = right_t.at[lines, source]
-
-        @functools.partial(each, last=width_l // wide)
-        def _(n):
-            value = jnp.dot(lhs[...], left[left_rows, pl.ds(pl.multiple_of(n * wide, wide), wide)], preferred_element_type=jnp.float32)
+    def product(into, lines, source, left, left_rows, size, wide, add):
+        for n in range(width_l // wide):
+            value = jnp.dot(right_t[lines, source], left[left_rows, pl.ds(n * wide, wide)], preferred_element_type=jnp.float32)
             for one in range(wide // 128):
                 some = value[:, one * 128:(one + 1) * 128]
                 slab = n * (wide // 128) + one
                 into[slab, size, :] = into[slab, size, :] + some if add else some
 
-    def product_all(at, add):
+    def product_all(at, add, first=0, depth=rows):
         every = pl.ds(0, width_r)
-        product(acc, every, block(at), left_full, block(at), every, add)
+        product(acc, every, block(at, first, depth), left_full, block(at, first, depth), every, 256, add)
 
     def product_one(at, q):
-        product(acc, cols(q), block(at), left_full, block(at), cols(q), True)
+        product(acc, cols(q), block(at), left_full, block(at), cols(q), 512, True)
 
     def project(source, first_row):
         for eq in range(CH // 4):
@@ -500,46 +493,50 @@
     own.wait()
     each(lambda q: turn(zc, q))
 
-    @each
-    def _(p):
-        arrived(right_slot(zc - 1, p), in_recv.at[0, p])
-        when(inner)(lambda: fwd_copy(1, p).start())
-        arrived(y_slot(1 - yc, 0, p, k), y_recv.at[0, p])
-        s_copy(0, p).start()
-        when(end, yc == 1)(lambda: far_copy(p).start())
-
-        @when(inner, p >= 1)
-        def _():
-            arrived(far_slot(p - 1, k), far_recv.at[p - 1])
-            share_copy(p - 1).start()
-
-        turn(zc - 1, p)
-
-    when(end, yc == 1)(lambda: each(lambda q: end_copy(q).start(), 1))
-
     def end_arrived(q):
         arrived(right_slot(3, q), end_recv.at[q])
         fwd_copy(-1, q).start()
         turn(3, q)
 
-    when(inner)(lambda: end_arrived(0))
+    def share(p):
+        arrived(far_slot(p, k), far_recv.at[p])
+        share_copy(p).start()
+
+    @each
+    def _(p):
+        arrived(y_slot(1 - yc, 0, p, k), y_recv.at[0, p])
+        s_copy(0, p).start()
+        when(end, yc == 1)(lambda: far_copy(p).start())
+        arrived(right_slot(zc - 1, p), in_recv.at[0, p])
+        when(inner)(lambda: fwd_copy(1, p).start())
+        turn(zc - 1, p)
+        when(inner, p >= 1, p <= early)(lambda: end_arrived(p - 1))
+
+    when(end, yc == 1)(lambda: each(lambda q: end_copy(q).start(), early))
+    when(inner)(lambda: each(share, 0, early))
     each(lambda p: arrived(y_slot(1 - yc, 0, p, 1 - k), s_recv.at[0, p]))
-    product_all(2, False)
-    near, late = 1 + 2 * yc, 3 - 2 * yc
+    is_inner = 3 - zc
+    product_all(is_inner * (1 + yc) + (1 - is_inner) * 3, False)
+    near, late = is_inner * 3 + (1 - is_inner) * (1 + yc), 2 - yc
 
     def far(q):
         arrived(right_slot(0, q), in_recv.at[1, q])
         turn(0, q)
-        product(acc_far, cols(q), block(0), left_far, pl.ds(0, rows), pl.ds(0, TILE), False)
+        product(acc_far, cols(q), block(0), left_far, pl.ds(0, rows), pl.ds(0, TILE), 512, False)
         part[q] = project(acc_far, 0).astype(part.dtype)
+        part_copy(q).start()
         product_one(0, q)
-        part_copy(q).start()
+
+    def late_half(at):
+        each(lambda p: arrived(y_slot(1 - yc, 1, p, 1 - k), s_recv.at[1, p]), at * steps // 2, (at + 1) * steps // 2)
+        product_all(late, True, at * (rows // 2), rows // 2)
 
     @each
     def _(q):
-        when(inner, q >= 1)(lambda: end_arrived(q))
+        when(inner, q >= early)(lambda: end_arrived(q))
         arrived(y_slot(1 - yc, 1, q, k), y_recv.at[1, q])
         s_copy(1, q).start()
+        when(inner, q < steps - early)(lambda: share(q + early))
 
         @when(end)
         def _():
@@ -547,21 +544,16 @@
             turn(1, q)
 
         product_one(near, q)
-
-        @when(inner, q == 0)
-        def _():
-            arrived(far_slot(steps - 1, k), far_recv.at[steps - 1])
-            share_copy(steps - 1).start()
-            each(lambda p: arrived(far_slot(p, 1 - k), a_recv.at[p]))
-
+        when(inner, q == steps - early - 1)(lambda: each(lambda p: arrived(far_slot(p, 1 - k), a_recv.at[p])))
         when(inner, q >= 1)(lambda: far(q - 1))
-
-    each(lambda p: arrived(y_slot(1 - yc, 1, p, 1 - k), s_recv.at[1, p]))
-    product_all(late, True)
+        when(inner, q == early)(lambda: late_half(0))
+
+    when(end)(lambda: late_half(0))
+    late_half(1)
 
     @each
     def _(q):
-        when(inner, q == steps - 1)(lambda: far(q))
+        when(inner, q == 1)(lambda: far(steps - 1))
         value = project(acc, q * TILE)
         for i in range(4):
             out_v[q, :, i] = value[i * quads * heads:(i + 1) * quads * heads].reshape(quads, heads, 128)

time: 77.9 us -> 70.7 us (0.908)
  Pallas kernels: 75.4 us -> 68.3 us
    pallas_call x1, Pallas kernels: 75.4 us -> 68.3 us  [folded_call(): pl.pallas_call(folded, out_shape=jax.ShapeDtypeStruct((left_dev, right_de...]
where the time goes in v2:
time: 70.7 us; the launch traced here: 70.6 us
  Pallas kernels  68.3 us (97%)
  local copies, waits for them, and re-layouts  2.26 us (3%)
    pallas_call x1, Pallas kernels, folded_call(): pl.pallas_call(folded, out_shape=jax.ShapeDtypeStruct((left_dev, right_de...  68.3 us
    unnamed x1, local copies, waits for them, and re-layouts  2.26 us

profile of v2, /device:TPU:0, one launch (start us, length us, event | category | flops | bytes accessed | tf_op | source)
XLA Modules:
  0.0 70.6 jit_solution(10380384553229600305)
XLA Ops:
  0.0 68.3 %pair_mean.1 = f32[64,32,128]{2,1,0:T(8,128)} custom-call(bf16[512,2048]{1,0:T(8,128)(2,1)} %left_ref.1, bf16[512,1024]{1,0:T(8,128)(2,1)} %right_ref.1, s32[32,64]{1,0:T(8,128)} %bitcast.1, bf16[1024,128]{1,0:T(8,128)(2,1)} %w_hbm.1), custom_call_target="tpu_custom_call" | custom-call | tf_op jit(solution)/shard_map/pair_mean/pallas_call | solution.py:601
  68.3 2.3 %copy.6 = f32[64,32,128]{2,1,0:T(8,128)} copy(f32[64,32,128]{2,1,0:T(8,128)} %pair_mean.1) | data formatting | bytes 2097152

commit v3 on v2

--- a/solution.py
+++ b/solution.py
@@ -292,8 +292,8 @@
 
 
 def folded(left_ref, right_ref, counts_ref, w_hbm, out_ref, w_in, w_wide, w_ref, counts_in, cover, order, left_full, left_far, right_full, right_t,
-           acc, acc_far, flat, part, out_v, in_send, in_recv, fwd_send, far_send, far_recv, end_send, end_recv, own_send, own_recv,
-           y_send, y_recv, s_send, s_recv, a_send, a_recv, p_send, p_recv, own_sem, out_sem):
+           acc, acc_far, flat, part, out_v, in_send, in_recv, fwd_send, mid_send, mid_recv, far_send, far_recv, end_send, end_recv, own_send, own_recv,
+           y_send, y_recv, s_send, s_recv, a_send, a_recv, p_send, p_recv, own_sem):
     rows, width_l = left_ref.shape
     width_r = right_ref.shape[1]
     steps = width_r // TILE
@@ -354,12 +354,24 @@
     def in_copy(way, q):
         return remote(right_ref.at[:, cols(q)], right_slot(2, q), in_send.at[(way + 1) // 2, q], in_recv.at[0, q], z_dev(way))
 
-    def fwd_copy(way, q):
-        slot = right_slot(3 if way < 0 else 1, q)
-        return remote(slot, slot, fwd_send.at[(way + 1) // 2, q], in_recv.at[1, q], z_dev(way))
-
-    def end_copy(q):
-        return remote(right_ref.at[:, cols(q)], right_slot(3, q), end_send.at[q], end_recv.at[q], z_dev(-1))
+    def fwd_copy(q):
+        slot = right_slot(1, q)
+        return remote(slot, slot, fwd_send.at[q], in_recv.at[1, q], z_dev(1))
+
+    def half_slot(at, q, h):
+        return right_full.at[block(at, h * (rows // 2), rows // 2), cols(q)]
+
+    def mid_copy(q, h):
+        slot = half_slot(3, q, h)
+        return remote(slot, slot, mid_send.at[q, h], mid_recv.at[q, h], z_dev(-1))
+
+    def end_copy(q, h):
+        source = right_ref.at[pl.ds(h * (rows // 2), rows // 2), cols(q)]
+        return remote(source, half_slot(3, q, h), end_send.at[q, h], end_recv.at[q, h], z_dev(-1))
+
+    def end_start(q):
+        for h in range(2):
+            end_copy(q, h).start()
 
     def own_half():
         return pl.ds(pl.multiple_of(k * half, half), half)
@@ -416,7 +428,7 @@
             in_copy(-1, q).start()
             in_copy(1, q).start()
 
-    when(end)(lambda: each(lambda q: end_copy(q).start(), 0, early))
+    when(end)(lambda: each(end_start, 0, early))
     own_left = pltpu.make_async_copy(left_ref, left_full.at[pl.ds(pl.multiple_of(r * rows, rows), rows), :], own_sem.at[0])
     own = pltpu.make_async_copy(right_ref, right_full.at[block(zc), :], own_sem.at[1])
     weights = pltpu.make_async_copy(w_hbm, w_in, own_sem.at[2])
@@ -434,7 +446,7 @@
     own_left.wait()
     when(end, yc == 0, kc == 0)(lambda: each(lambda p: far_copy(p).start()))
     each(lambda p: y_copy(1, p).start())
-    when(end, yc == 0)(lambda: each(lambda q: end_copy(q).start(), early))
+    when(end, yc == 0)(lambda: each(end_start, early))
 
     row = lax.broadcasted_iota(jnp.int32, (TILE, TILE), 0)
     column = lax.broadcasted_iota(jnp.int32, (TILE, TILE), 1)
@@ -483,19 +495,19 @@
             if add:
                 more = part[q, pl.ds(i * quads * heads, quads * heads), :]
                 value = value + more.astype(jnp.float32).reshape(value.shape)
-            out_v[q, :, i] = value / cover[:, i, pl.ds(pl.multiple_of(q * heads, heads), heads), :]
-        out_copy(q).start()
-
-    def out_copy(q):
-        at = pl.ds(pl.multiple_of(q * heads, heads), heads)
-        return pltpu.make_async_copy(out_v.at[q].reshape(4 * quads, heads, 128), out_ref.at[:, at, :], out_sem.at[q])
+            at = pl.ds(pl.multiple_of(q * heads, heads), heads)
+            out_ref[pl.ds(i, quads, stride=4), at, :] = value / cover[:, i, at, :]
 
     own.wait()
     each(lambda q: turn(zc, q))
 
+    def pass_on(q, h):
+        arrived(half_slot(3, q, h), end_recv.at[q, h])
+        mid_copy(q, h).start()
+
     def end_arrived(q):
-        arrived(right_slot(3, q), end_recv.at[q])
-        fwd_copy(-1, q).start()
+        for h in range(2):
+            pass_on(q, h)
         turn(3, q)
 
     def share(p):
@@ -508,85 +520,116 @@
         s_copy(0, p).start()
         when(end, yc == 1)(lambda: far_copy(p).start())
         arrived(right_slot(zc - 1, p), in_recv.at[0, p])
-        when(inner)(lambda: fwd_copy(1, p).start())
+        when(inner)(lambda: fwd_copy(p).start())
         turn(zc - 1, p)
         when(inner, p >= 1, p <= early)(lambda: end_arrived(p - 1))
 
-    when(end, yc == 1)(lambda: each(lambda q: end_copy(q).start(), early))
-    when(inner)(lambda: each(share, 0, early))
+    when(end, yc == 1)(lambda: each(end_start, early))
     each(lambda p: arrived(y_slot(1 - yc, 0, p, 1 - k), s_recv.at[0, p]))
-    is_inner = 3 - zc
-    product_all(is_inner * (1 + yc) + (1 - is_inner) * 3, False)
-    near, late = is_inner * 3 + (1 - is_inner) * (1 + yc), 2 - yc
-
-    def far(q):
-        arrived(right_slot(0, q), in_recv.at[1, q])
-        turn(0, q)
-        product(acc_far, cols(q), block(0), left_far, pl.ds(0, rows), pl.ds(0, TILE), 512, False)
-        part[q] = project(acc_far, 0).astype(part.dtype)
-        part_copy(q).start()
-        product_one(0, q)
+    late = 2 - yc
+
+    def y_arrived(p):
+        arrived(y_slot(1 - yc, 1, p, k), y_recv.at[1, p])
+        s_copy(1, p).start()
 
     def late_half(at):
         each(lambda p: arrived(y_slot(1 - yc, 1, p, 1 - k), s_recv.at[1, p]), at * steps // 2, (at + 1) * steps // 2)
         product_all(late, True, at * (rows // 2), rows // 2)
 
-    @each
-    def _(q):
-        when(inner, q >= early)(lambda: end_arrived(q))
-        arrived(y_slot(1 - yc, 1, q, k), y_recv.at[1, q])
-        s_copy(1, q).start()
-        when(inner, q < steps - early)(lambda: share(q + early))
-
-        @when(end)
-        def _():
-            arrived(right_slot(1, q), in_recv.at[1, q])
-            turn(1, q)
-
-        product_one(near, q)
-        when(inner, q == steps - early - 1)(lambda: each(lambda p: arrived(far_slot(p, 1 - k), a_recv.at[p])))
-        when(inner, q >= 1)(lambda: far(q - 1))
-        when(inner, q == early)(lambda: late_half(0))
-
-    when(end)(lambda: late_half(0))
-    late_half(1)
-
-    @each
-    def _(q):
-        when(inner, q == 1)(lambda: far(steps - 1))
+    def far_product(q):
+        for h in range(2):
+            arrived(half_slot(0, q, h), mid_recv.at[q, h])
+        turn(0, q)
+        product(acc_far, cols(q), block(0), left_far, pl.ds(0, rows), pl.ds(0, TILE), 512, False)
+
+    def far_send_on(q):
+        part[q] = project(acc_far, 0).astype(part.dtype)
+        part_copy(q).start()
+
+    def finish(q):
         value = project(acc, q * TILE)
         for i in range(4):
             out_v[q, :, i] = value[i * quads * heads:(i + 1) * quads * heads].reshape(quads, heads, 128)
-        when(inner)(lambda: settle(q, False))
+
+    def sent(q):
+        own_copy(q).wait_send()
+        for pos in range(2):
+            y_copy(pos, q).wait_send()
+            s_copy(pos, q).wait_send()
+
+    @when(inner)
+    def _():
+        each(share, 0, early)
+        product_all(1 + yc, False)
+        each(lambda q: product_one(3, q), 0, early)
+        each(y_arrived, 0, early - 1)
+        each(share, early)
+        y_arrived(early - 1)
+        each(lambda p: arrived(far_slot(p, 1 - k), a_recv.at[p]))
+        for q in range(early):
+            far_product(q)
+            far_send_on(q)
+            pass_on(early, q)
+            product_one(0, q)
+        turn(3, early)
+        y_arrived(early)
+        product_one(3, early)
+        pass_on(early + 1, 0)
+        late_half(0)
+        far_product(early)
+        pass_on(early + 1, 1)
+        far_send_on(early)
+        y_arrived(early + 1)
+        turn(3, early + 1)
+        product_one(3, early + 1)
+        product_one(0, early)
+        late_half(1)
+        far_product(early + 1)
+        far_send_on(early + 1)
+        product_one(0, early + 1)
+
+        @each
+        def _(q):
+            finish(q)
+            settle(q, False)
+
+        @each
+        def _(q):
+            sent(q)
+            for way in (-1, 1):
+                in_copy(way, q).wait_send()
+            fwd_copy(q).wait_send()
+            for h in range(2):
+                mid_copy(q, h).wait_send()
+            share_copy(q).wait_send()
+            part_copy(q).wait_send()
 
     @when(end)
     def _():
+        product_all(3, False)
+
+        @each
+        def _(q):
+            y_arrived(q)
+            arrived(right_slot(1, q), in_recv.at[1, q])
+            turn(1, q)
+            product_one(1 + yc, q)
+
+        late_half(0)
+        late_half(1)
+        each(finish)
+
+        @each
+        def _(q):
+            sent(q)
+            for h in range(2):
+                end_copy(q, h).wait_send()
+            far_copy(q).wait_send()
+
         @each
         def _(q):
             arrived(part.at[q], p_recv.at[q])
             settle(q, True)
-
-    @each
-    def _(q):
-        own_copy(q).wait_send()
-        for pos in range(2):
-            y_copy(pos, q).wait_send()
-            s_copy(pos, q).wait_send()
-
-        @when(inner)
-        def _():
-            for way in (-1, 1):
-                in_copy(way, q).wait_send()
-                fwd_copy(way, q).wait_send()
-            share_copy(q).wait_send()
-            part_copy(q).wait_send()
-
-        @when(end)
-        def _():
-            end_copy(q).wait_send()
-            far_copy(q).wait_send()
-
-        out_copy(q).wait()
 
 
 def folded_call(left_act, right_act, counts, w_out):
@@ -602,7 +645,7 @@
         folded,
         out_shape=jax.ShapeDtypeStruct((left_dev, right_dev, pair), jnp.float32),
         in_specs=[pl.BlockSpec(memory_space=pl.ANY)] * 4,
-        out_specs=pl.BlockSpec(memory_space=pl.ANY),
+        out_specs=pl.BlockSpec(memory_space=pltpu.VMEM),
         scratch_shapes=[
             pltpu.VMEM(w_out.shape, w_out.dtype),
             pltpu.VMEM(w_out.shape, jnp.float32),
@@ -619,13 +662,14 @@
             pltpu.VMEM((left_dev * heads, CH * CH), jnp.bfloat16),
             pltpu.VMEM((steps, left_dev * heads, pair), jnp.bfloat16),
             pltpu.VMEM((steps, left_dev // 4, 4, heads, pair), jnp.float32),
-            dma((2, steps)), dma((2, steps)), dma((2, steps)), dma((steps,)), dma((steps,)), dma((steps,)), dma((steps,)), dma((steps,)),
+            dma((2, steps)), dma((2, steps)), dma((steps,)), dma((steps, 2)), dma((steps, 2)), dma((steps,)), dma((steps,)),
+            dma((steps, 2)), dma((steps, 2)), dma((steps,)),
             dma((steps,)), dma((2, steps)), dma((2, steps)), dma((2, steps)), dma((2, steps)), dma((steps,)), dma((steps,)), dma((steps,)),
-            dma((steps,)), dma((4,)), dma((steps,)),
+            dma((steps,)), dma((4,)),
         ],
-        compiler_params=pltpu.CompilerParams(collective_id=0, has_side_effects=True, vmem_limit_bytes=56 * 1024 * 1024),
+        compiler_params=pltpu.CompilerParams(collective_id=0, has_side_effects=True, vmem_limit_bytes=38000 * 1024),
         name="pair_mean",
-    )(left_act, right_act, counts.T, w_out)
+    )(*(pltpu.with_memory_space_constraint(x, pltpu.HBM) for x in (left_act, right_act, counts.T, w_out)))
 
 
 def solution(mesh):

time: 70.7 us -> 67.1 us (0.949)
  Pallas kernels: 68.3 us -> 66 us
  local copies, waits for them, and re-layouts: 2.26 us -> 0.97 us
    pallas_call x1, Pallas kernels: 68.3 us -> 66 us  [folded_call(): pl.pallas_call(folded, out_shape=jax.ShapeDtypeStruct((left_dev, right_de...]
    unnamed x1, local copies, waits for them, and re-layouts: 2.26 us -> 0.97 us
where the time goes in v3:
time: 67.1 us; the launch traced here: 67 us
  Pallas kernels  66 us (98%)
  local copies, waits for them, and re-layouts  0.97 us (1%)
    pallas_call x1, Pallas kernels, folded_call(): pl.pallas_call(folded, out_shape=jax.ShapeDtypeStruct((left_dev, right_de...  66 us

profile of v3, /device:TPU:0, one launch (start us, length us, event | category | flops | bytes accessed | tf_op | source)
XLA Modules:
  0.0 67.0 jit_solution(4111104627448198937)
XLA Ops:
  0.0 66.0 %pair_mean.1 = f32[64,32,128]{2,1,0:T(8,128)S(1)} custom-call(bf16[512,2048]{1,0:T(8,128)(2,1)} %left_ref.1, bf16[512,1024]{1,0:T(8,128)(2,1)} %right_ref.1, s32[32,64]{1,0:T(8,128)} %bitcast.1, bf16[1024,128]{1,0:T(8,128)(2,1)} %w_hbm.1), custom_call_target="tpu_custom_call" | custom-call | tf_op jit(solution)/shard_map/pair_mean/pallas_call | solution.py:644
  66.0 1.0 %copy.6 = f32[64,32,128]{2,1,0:T(8,128)} copy(f32[64,32,128]{2,1,0:T(8,128)S(1)} %pair_mean.1) | data formatting | bytes 2097152

commit v4 on v3

--- a/solution.py
+++ b/solution.py
@@ -292,8 +292,7 @@
 
 
 def folded(left_ref, right_ref, counts_ref, w_hbm, out_ref, w_in, w_wide, w_ref, counts_in, cover, order, left_full, left_far, right_full, right_t,
-           acc, acc_far, flat, part, out_v, in_send, in_recv, fwd_send, mid_send, mid_recv, far_send, far_recv, end_send, end_recv, own_send, own_recv,
-           y_send, y_recv, s_send, s_recv, a_send, a_recv, p_send, p_recv, own_sem):
+           acc, acc_far, flat, part, out_v, send, in_recv, far_recv, end_recv, own_recv, y_recv, s_recv, a_recv, own_sem):
     rows, width_l = left_ref.shape
     width_r = right_ref.shape[1]
     steps = width_r // TILE
@@ -352,22 +351,22 @@
         return right_full.at[block(at), cols(q)]
 
     def in_copy(way, q):
-        return remote(right_ref.at[:, cols(q)], right_slot(2, q), in_send.at[(way + 1) // 2, q], in_recv.at[0, q], z_dev(way))
+        return remote(right_ref.at[:, cols(q)], right_slot(2, q), send.at[(way + 1) // 2], in_recv.at[0, q], z_dev(way))
 
     def fwd_copy(q):
         slot = right_slot(1, q)
-        return remote(slot, slot, fwd_send.at[q], in_recv.at[1, q], z_dev(1))
+        return remote(slot, slot, send.at[2], in_recv.at[1, q], z_dev(1))
 
     def half_slot(at, q, h):
         return right_full.at[block(at, h * (rows // 2), rows // 2), cols(q)]
 
     def mid_copy(q, h):
         slot = half_slot(3, q, h)
-        return remote(slot, slot, mid_send.at[q, h], mid_recv.at[q, h], z_dev(-1))
+        return remote(slot, slot, send.at[3], in_recv.at[1, q], z_dev(-1))
 
     def end_copy(q, h):
         source = right_ref.at[pl.ds(h * (rows // 2), rows // 2), cols(q)]
-        return remote(source, half_slot(3, q, h), end_send.at[q, h], end_recv.at[q, h], z_dev(-1))
+        return remote(source, half_slot(3, q, h), send.at[3], end_recv.at[q, h], z_dev(-1))
 
     def end_start(q):
         for h in range(2):
@@ -378,38 +377,38 @@
 
     def far_copy(p):
         at = pl.ds(pl.multiple_of(p * piece, piece), piece)
-        return remote(left_full.at[block(0, p * piece, piece), own_half()], left_far.at[at, own_half()], far_send.at[p], far_recv.at[p], z_dev(-1))
+        return remote(left_full.at[block(0, p * piece, piece), own_half()], left_far.at[at, own_half()], send.at[2], far_recv.at[p], z_dev(-1))
 
     def far_slot(p, core):
         return left_far.at[pl.ds(pl.multiple_of(p * piece, piece), piece), pl.ds(pl.multiple_of(core * half, half), half)]
 
     def share_copy(p):
-        return remote(far_slot(p, k), far_slot(p, k), a_send.at[p], a_recv.at[p], sib_dev)
+        return remote(far_slot(p, k), far_slot(p, k), send.at[4], a_recv.at[0], sib_dev)
 
     def own_copy(p):
         at = pl.ds(pl.multiple_of(p * piece, piece), piece)
         slot = left_full.at[pl.ds(pl.multiple_of(r * rows + p * piece, piece), piece), :]
-        return remote(left_ref.at[at, :], slot, own_send.at[p], own_recv.at[p], sib_dev)
+        return remote(left_ref.at[at, :], slot, send.at[5], own_recv.at[p], sib_dev)
 
     def own_arrived(p):
         other = r + 1 - 2 * k
         arrived(left_full.at[pl.ds(pl.multiple_of(other * rows + p * piece, piece), piece), :], own_recv.at[p])
 
-    def y_slot(side, pos, p, core):
+    def y_slot(side, pos, p, core, count=1):
         at = 3 * side if pos == 0 else 1 + side
-        return left_full.at[block(at, p * piece, piece), pl.ds(pl.multiple_of(core * half, half), half)]
+        return left_full.at[block(at, p * piece, count * piece), pl.ds(pl.multiple_of(core * half, half), half)]
 
     def y_copy(pos, p, own=False):
         slot = y_slot(yc, pos, p, k)
         source = left_ref.at[pl.ds(pl.multiple_of(p * piece, piece), piece), own_half()] if own else slot
-        return remote(source, slot, y_send.at[pos, p], y_recv.at[pos, p], y_dev)
-
-    def s_copy(pos, p):
+        return remote(source, slot, send.at[6], y_recv.at[pos, p], y_dev)
+
+    def s_copy(pos, p, group):
         slot = y_slot(1 - yc, pos, p, k)
-        return remote(slot, slot, s_send.at[pos, p], s_recv.at[pos, p], sib_dev)
+        return remote(slot, slot, send.at[7], s_recv.at[group], sib_dev)
 
     def part_copy(q):
-        return remote(part.at[q], part.at[q], p_send.at[q], p_recv.at[q], z_dev(1))
+        return remote(part.at[q], part.at[q], send.at[8], far_recv.at[q], z_dev(1))
 
     def each(body, first=0, last=steps):
         def step(at, carry):
@@ -417,9 +416,6 @@
             return carry
 
         lax.fori_loop(first, last, step, 0)
-
-    first = kc == yc
-    when(first)(lambda: each(lambda p: y_copy(0, p, True).start()))
 
     @when(inner)
     def _():
@@ -429,6 +425,8 @@
             in_copy(1, q).start()
 
     when(end)(lambda: each(end_start, 0, early))
+    first = kc == yc
+    when(first)(lambda: each(lambda p: y_copy(0, p, True).start()))
     own_left = pltpu.make_async_copy(left_ref, left_full.at[pl.ds(pl.multiple_of(r * rows, rows), rows), :], own_sem.at[0])
     own = pltpu.make_async_copy(right_ref, right_full.at[block(zc), :], own_sem.at[1])
     weights = pltpu.make_async_copy(w_hbm, w_in, own_sem.at[2])
@@ -517,7 +515,7 @@
     @each
     def _(p):
         arrived(y_slot(1 - yc, 0, p, k), y_recv.at[0, p])
-        s_copy(0, p).start()
+        s_copy(0, p, 0).start()
         when(end, yc == 1)(lambda: far_copy(p).start())
         arrived(right_slot(zc - 1, p), in_recv.at[0, p])
         when(inner)(lambda: fwd_copy(p).start())
@@ -525,20 +523,22 @@
         when(inner, p >= 1, p <= early)(lambda: end_arrived(p - 1))
 
     when(end, yc == 1)(lambda: each(end_start, early))
-    each(lambda p: arrived(y_slot(1 - yc, 0, p, 1 - k), s_recv.at[0, p]))
+    arrived(y_slot(1 - yc, 0, 0, 1 - k, steps), s_recv.at[0])
     late = 2 - yc
+    groups = ((0, early), (early, early + 1), (early + 1, steps))
 
     def y_arrived(p):
+        group = next(at for at, (_, last) in enumerate(groups) if p < last)
         arrived(y_slot(1 - yc, 1, p, k), y_recv.at[1, p])
-        s_copy(1, p).start()
-
-    def late_half(at):
-        each(lambda p: arrived(y_slot(1 - yc, 1, p, 1 - k), s_recv.at[1, p]), at * steps // 2, (at + 1) * steps // 2)
-        product_all(late, True, at * (rows // 2), rows // 2)
+        s_copy(1, p, 1 + group).start()
+
+    def late_part(group):
+        low, high = groups[group]
+        arrived(y_slot(1 - yc, 1, low, 1 - k, high - low), s_recv.at[1 + group])
+        product_all(late, True, low * piece, (high - low) * piece)
 
     def far_product(q):
-        for h in range(2):
-            arrived(half_slot(0, q, h), mid_recv.at[q, h])
+        arrived(right_slot(0, q), in_recv.at[1, q])
         turn(0, q)
         product(acc_far, cols(q), block(0), left_far, pl.ds(0, rows), pl.ds(0, TILE), 512, False)
 
@@ -551,84 +551,81 @@
         for i in range(4):
             out_v[q, :, i] = value[i * quads * heads:(i + 1) * quads * heads].reshape(quads, heads, 128)
 
-    def sent(q):
-        own_copy(q).wait_send()
-        for pos in range(2):
-            y_copy(pos, q).wait_send()
-            s_copy(pos, q).wait_send()
+    def sent(sem, count=1):
+        slot = left_full.at[pl.ds(0, count * rows), pl.ds(0, half)]
+        arrived(slot, send.at[sem])
 
     @when(inner)
     def _():
         each(share, 0, early)
         product_all(1 + yc, False)
-        each(lambda q: product_one(3, q), 0, early)
-        each(y_arrived, 0, early - 1)
+        for q in range(early):
+            product_one(3, q)
+        y_arrived(0)
         each(share, early)
-        y_arrived(early - 1)
-        each(lambda p: arrived(far_slot(p, 1 - k), a_recv.at[p]))
-        for q in range(early):
-            far_product(q)
-            far_send_on(q)
-            pass_on(early, q)
-            product_one(0, q)
-        turn(3, early)
-        y_arrived(early)
-        product_one(3, early)
-        pass_on(early + 1, 0)
-        late_half(0)
-        far_product(early)
-        pass_on(early + 1, 1)
-        far_send_on(early)
-        y_arrived(early + 1)
-        turn(3, early + 1)
-        product_one(3, early + 1)
-        product_one(0, early)
-        late_half(1)
-        far_product(early + 1)
-        far_send_on(early + 1)
-        product_one(0, early + 1)
+        arrived(left_far.at[:, pl.ds(pl.multiple_of((1 - k) * half, half), half)], a_recv.at[0])
+        far_product(0)
+        y_arrived(1)
+        far_send_on(0)
+        pass_on(2, 0)
+        product_one(0, 0)
+        far_product(1)
+        far_send_on(1)
+        pass_on(2, 1)
+        product_one(0, 1)
+        turn(3, 2)
+        y_arrived(2)
+        product_one(3, 2)
+        pass_on(3, 0)
+        late_part(0)
+        late_part(1)
+        pass_on(3, 1)
+        far_product(2)
+        y_arrived(3)
+        far_send_on(2)
+        turn(3, 3)
+        product_one(3, 3)
+        product_one(0, 2)
+        late_part(2)
+        far_product(3)
+        far_send_on(3)
+        product_one(0, 3)
 
         @each
         def _(q):
             finish(q)
             settle(q, False)
 
-        @each
-        def _(q):
-            sent(q)
-            for way in (-1, 1):
-                in_copy(way, q).wait_send()
-            fwd_copy(q).wait_send()
-            for h in range(2):
-                mid_copy(q, h).wait_send()
-            share_copy(q).wait_send()
-            part_copy(q).wait_send()
+        sent(0)
+        sent(1)
+        sent(2)
+        sent(3)
+        sent(4)
+        sent(5, 2)
+        sent(6, 2)
+        sent(7, 2)
+        arrived(part, send.at[8])
 
     @when(end)
     def _():
         product_all(3, False)
-
-        @each
-        def _(q):
+        for q in range(steps):
             y_arrived(q)
             arrived(right_slot(1, q), in_recv.at[1, q])
             turn(1, q)
             product_one(1 + yc, q)
-
-        late_half(0)
-        late_half(1)
+        for group in range(len(groups)):
+            late_part(group)
         each(finish)
+        sent(2)
+        sent(3)
+        sent(5, 2)
+        sent(6, 2)
+        sent(7, 2)
 
         @each
         def _(q):
-            sent(q)
-            for h in range(2):
-                end_copy(q, h).wait_send()
-            far_copy(q).wait_send()
-
-        @each
-        def _(q):
-            arrived(part.at[q], p_recv.at[q])
+            arrived(part.at[q], far_recv.at[q])
             settle(q, True)
 
 
@@ -662,10 +659,7 @@
             pltpu.VMEM((left_dev * heads, CH * CH), jnp.bfloat16),
             pltpu.VMEM((steps, left_dev * heads, pair), jnp.bfloat16),
             pltpu.VMEM((steps, left_dev // 4, 4, heads, pair), jnp.float32),
-            dma((2, steps)), dma((2, steps)), dma((steps,)), dma((steps, 2)), dma((steps, 2)), dma((steps,)), dma((steps,)),
-            dma((steps, 2)), dma((steps, 2)), dma((steps,)),
-            dma((steps,)), dma((2, steps)), dma((2, steps)), dma((2, steps)), dma((2, steps)), dma((steps,)), dma((steps,)), dma((steps,)),
-            dma((steps,)), dma((4,)),
+            dma((9,)), dma((2, steps)), dma((steps,)), dma((steps, 2)), dma((steps,)), dma((2, steps)), dma((4,)), dma((1,)), dma((4,)),
         ],
         compiler_params=pltpu.CompilerParams(collective_id=0, has_side_effects=True, vmem_limit_bytes=38000 * 1024),
         name="pair_mean",
@@ -677,7 +671,8 @@
     n_y = n_r // CORES
 
     def shards(left_act, right_act, counts, w_out):
-        if (n_z, n_y) == (4, 2):
+        width_l, width_r = left_act.shape[1], right_act.shape[1]
+        if (n_z, n_y) == (4, 2) and width_r == 4 * TILE and width_l == CORES * width_r:
             return folded_call(left_act, right_act, counts, w_out)
         rows_l, width_l = left_act.shape
         rows_r, width_r = right_act.shape

time: 67.1 us -> 66.3 us (0.988)
  Pallas kernels: 66 us -> 65.2 us
    pallas_call x1, Pallas kernels: 66 us -> 65.2 us  [folded_call(): pl.pallas_call(folded, out_shape=jax.ShapeDtypeStruct((left_dev, right_de...]
where the time goes in v4:
time: 66.3 us; the launch traced here: 66.2 us
  Pallas kernels  65.2 us (98%)
  local copies, waits for them, and re-layouts  0.97 us (1%)
    pallas_call x1, Pallas kernels, folded_call(): pl.pallas_call(folded, out_shape=jax.ShapeDtypeStruct((left_dev, right_de...  65.2 us

profile of v4, /device:TPU:0, one launch (start us, length us, event | category | flops | bytes accessed | tf_op | source)
XLA Modules:
  0.0 66.2 jit_solution(3598830932910062938)
XLA Ops:
  0.0 65.2 %pair_mean.1 = f32[64,32,128]{2,1,0:T(8,128)S(1)} custom-call(bf16[512,2048]{1,0:T(8,128)(2,1)} %left_ref.1, bf16[512,1024]{1,0:T(8,128)(2,1)} %right_ref.1, s32[32,64]{1,0:T(8,128)} %bitcast.1, bf16[1024,128]{1,0:T(8,128)(2,1)} %w_hbm.1), custom_call_target="tpu_custom_call" | custom-call | tf_op jit(solution)/shard_map/pair_mean/pallas_call | solution.py:641
  65.2 1.0 %copy.6 = f32[64,32,128]{2,1,0:T(8,128)} copy(f32[64,32,128]{2,1,0:T(8,128)S(1)} %pair_mean.1) | data formatting | bytes 2097152

commit v5 on v4

--- a/solution.py
+++ b/solution.py
@@ -300,6 +300,8 @@
     half = width_l // CORES
     quads = width_l // 128
     heads = TILE // CH
+    pair = w_hbm.shape[1]
+    lines = quads * heads
     early = steps // 2
     z = lax.axis_index("left")
     r = lax.axis_index("right")
@@ -452,7 +454,10 @@
     weights.wait()
     w_wide[...] = w_in[...].astype(jnp.float32)
     for e in range(CH):
-        w_ref[pl.ds(e * CH, CH), :] = w_wide[pl.ds(e, CH, stride=CH), :].astype(w_ref.dtype)
+        some = w_wide[pl.ds(e, CH, stride=CH), :].astype(w_ref.dtype)
+        for i in range(2):
+            w_ref[pl.ds((2 * e + i) * CH, CH), i * pair:(i + 1) * pair] = some
+            w_ref[pl.ds((2 * e + i) * CH, CH), (1 - i) * pair:(2 - i) * pair] = jnp.zeros_like(some)
     counts_copy.wait()
     counted = counts_in[...].astype(jnp.float32)
     for i in range(counted.shape[1]):
@@ -478,21 +483,25 @@
         product(acc, cols(q), block(at), left_full, block(at), cols(q), 512, True)
 
     def project(source, first_row):
-        for eq in range(CH // 4):
-            tiles = []
-            for e in range(4):
-                tile = source[:, pl.ds(pl.multiple_of(first_row + (eq * 4 + e) * heads, heads), heads), :]
-                tiles.append(tile.reshape(quads * heads, 128).astype(flat.dtype))
-            for i, value in enumerate(lane_quads(tiles)):
-                flat[pl.ds(i * quads * heads, quads * heads), pl.ds(eq * 128, 128)] = value
+        low = lax.broadcasted_iota(jnp.int32, (lines, 128), 1) < 64
+        for two in range(CH // 2):
+            a, b = (
+                source[:, pl.ds(pl.multiple_of(first_row + e * heads, heads), heads), :].reshape(lines, 128).astype(flat.dtype)
+                for e in (2 * two, 2 * two + 1)
+            )
+            at = pl.ds(two * 128, 128)
+            flat[pl.ds(0, lines), at] = jnp.where(low, a, pltpu.roll(b, 64, 1))
+            flat[pl.ds(lines, lines), at] = jnp.where(low, pltpu.roll(a, 64, 1), b)
         return jnp.dot(flat[...], w_ref[...], preferred_element_type=jnp.float32)
+
+    def spot(i):
+        return slice(i // 2 * lines, (i // 2 + 1) * lines), slice(i % 2 * pair, (i % 2 + 1) * pair)
 
     def settle(q, add):
         for i in range(4):
             value = out_v[q, :, i]
             if add:
-                more = part[q, pl.ds(i * quads * heads, quads * heads), :]
-                value = value + more.astype(jnp.float32).reshape(value.shape)
+                value = value + part[(q, *spot(i))].astype(jnp.float32).reshape(value.shape)
             at = pl.ds(pl.multiple_of(q * heads, heads), heads)
             out_ref[pl.ds(i, quads, stride=4), at, :] = value / cover[:, i, at, :]
 
@@ -537,9 +546,11 @@
         arrived(y_slot(1 - yc, 1, low, 1 - k, high - low), s_recv.at[1 + group])
         product_all(late, True, low * piece, (high - low) * piece)
 
-    def far_product(q):
+    def far_turn(q):
         arrived(right_slot(0, q), in_recv.at[1, q])
         turn(0, q)
+
+    def far_product(q):
         product(acc_far, cols(q), block(0), left_far, pl.ds(0, rows), pl.ds(0, TILE), 512, False)
 
     def far_send_on(q):
@@ -549,7 +560,7 @@
     def finish(q):
         value = project(acc, q * TILE)
         for i in range(4):
-            out_v[q, :, i] = value[i * quads * heads:(i + 1) * quads * heads].reshape(quads, heads, 128)
+            out_v[q, :, i] = value[spot(i)].reshape(quads, heads, pair)
 
     def sent(sem, count=1):
         slot = left_full.at[pl.ds(0, count * rows), pl.ds(0, half)]
@@ -562,13 +573,16 @@
         for q in range(early):
             product_one(3, q)
         y_arrived(0)
-        each(share, early)
+        share(2)
+        far_turn(0)
+        product_one(0, 0)
+        share(3)
         arrived(left_far.at[:, pl.ds(pl.multiple_of((1 - k) * half, half), half)], a_recv.at[0])
         far_product(0)
         y_arrived(1)
         far_send_on(0)
         pass_on(2, 0)
-        product_one(0, 0)
+        far_turn(1)
         far_product(1)
         far_send_on(1)
         pass_on(2, 1)
@@ -580,15 +594,17 @@
         late_part(0)
         late_part(1)
         pass_on(3, 1)
+        far_turn(2)
         far_product(2)
         y_arrived(3)
         far_send_on(2)
         turn(3, 3)
         product_one(3, 3)
         product_one(0, 2)
-        late_part(2)
+        far_turn(3)
         far_product(3)
         far_send_on(3)
+        late_part(2)
         product_one(0, 3)
 
         @each
@@ -646,7 +662,7 @@
         scratch_shapes=[
             pltpu.VMEM(w_out.shape, w_out.dtype),
             pltpu.VMEM(w_out.shape, jnp.float32),
-            pltpu.VMEM(w_out.shape, w_out.dtype),
+            pltpu.VMEM((2 * w_out.shape[0], 2 * pair), w_out.dtype),
             pltpu.VMEM((right_dev, left_dev), counts.dtype),
             pltpu.VMEM((left_dev // 4, 4, right_dev, pair), jnp.float32),
             pltpu.VMEM((TILE, TILE), jnp.bfloat16),
@@ -656,8 +672,8 @@
             pltpu.VMEM((width_r, full), jnp.bfloat16),
             pltpu.VMEM((width_l // 128, width_r, 128), jnp.float32),
             pltpu.VMEM((width_l // 128, TILE, 128), jnp.float32),
-            pltpu.VMEM((left_dev * heads, CH * CH), jnp.bfloat16),
-            pltpu.VMEM((steps, left_dev * heads, pair), jnp.bfloat16),
+            pltpu.VMEM((left_dev * heads // 2, 2 * CH * CH), jnp.bfloat16),
+            pltpu.VMEM((steps, left_dev * heads // 2, 2 * pair), jnp.bfloat16),
             pltpu.VMEM((steps, left_dev // 4, 4, heads, pair), jnp.float32),
             dma((9,)), dma((2, steps)), dma((steps,)), dma((steps, 2)), dma((steps,)), dma((2, steps)), dma((4,)), dma((1,)), dma((4,)),
         ],

time: 66.3 us -> 64.8 us (0.977)
  Pallas kernels: 65.2 us -> 63.7 us
    pallas_call x1, Pallas kernels: 65.2 us -> 63.7 us  [folded_call(): pl.pallas_call(folded, out_shape=jax.ShapeDtypeStruct((left_dev, right_de...]
where the time goes in v5:
time: 64.8 us; the launch traced here: 64.7 us
  Pallas kernels  63.7 us (98%)
  local copies, waits for them, and re-layouts  0.97 us (1%)
    pallas_call x1, Pallas kernels, folded_call(): pl.pallas_call(folded, out_shape=jax.ShapeDtypeStruct((left_dev, right_de...  63.7 us

profile of v5, /device:TPU:0, one launch (start us, length us, event | category | flops | bytes accessed | tf_op | source)
XLA Modules:
  0.0 64.7 jit_solution(3973617200976039500)
XLA Ops:
  0.0 63.7 %pair_mean.1 = f32[64,32,128]{2,1,0:T(8,128)S(1)} custom-call(bf16[512,2048]{1,0:T(8,128)(2,1)} %left_ref.1, bf16[512,1024]{1,0:T(8,128)(2,1)} %right_ref.1, s32[32,64]{1,0:T(8,128)} %bitcast.1, bf16[1024,128]{1,0:T(8,128)(2,1)} %w_hbm.1), custom_call_target="tpu_custom_call" | custom-call | tf_op jit(solution)/shard_map/pair_mean/pallas_call | solution.py:657
  63.7 1.0 %copy.6 = f32[64,32,128]{2,1,0:T(8,128)} copy(f32[64,32,128]{2,1,0:T(8,128)S(1)} %pair_mean.1) | data formatting | bytes 2097152

commit v6 on v5

--- a/solution.py
+++ b/solution.py
@@ -359,20 +359,21 @@
         slot = right_slot(1, q)
         return remote(slot, slot, send.at[2], in_recv.at[1, q], z_dev(1))
 
-    def half_slot(at, q, h):
-        return right_full.at[block(at, h * (rows // 2), rows // 2), cols(q)]
-
-    def mid_copy(q, h):
-        slot = half_slot(3, q, h)
+    def cut(q):
+        return ((1, 0), (1, 1), (2, 2), (4, 4))[q]
+
+    def cut_slot(at, q, h, n):
+        return right_full.at[block(at, h * (rows // n), rows // n), cols(q)]
+
+    def mid_copy(q, h=0, n=1):
+        slot = cut_slot(3, q, h, n)
         return remote(slot, slot, send.at[3], in_recv.at[1, q], z_dev(-1))
 
-    def end_copy(q, h):
-        source = right_ref.at[pl.ds(h * (rows // 2), rows // 2), cols(q)]
-        return remote(source, half_slot(3, q, h), send.at[3], end_recv.at[q, h], z_dev(-1))
-
     def end_start(q):
-        for h in range(2):
-            end_copy(q, h).start()
+        n, at = cut(q)
+        for h in range(n):
+            source = right_ref.at[pl.ds(h * (rows // n), rows // n), cols(q)]
+            remote(source, cut_slot(3, q, h, n), send.at[3], end_recv.at[at + h], z_dev(-1)).start()
 
     def own_half():
         return pl.ds(pl.multiple_of(k * half, half), half)
@@ -426,7 +427,12 @@
             in_copy(-1, q).start()
             in_copy(1, q).start()
 
-    when(end)(lambda: each(end_start, 0, early))
+
+    @when(end)
+    def _():
+        end_start(0)
+        end_start(1)
+
     first = kc == yc
     when(first)(lambda: each(lambda p: y_copy(0, p, True).start()))
     own_left = pltpu.make_async_copy(left_ref, left_full.at[pl.ds(pl.multiple_of(r * rows, rows), rows), :], own_sem.at[0])
@@ -442,11 +448,18 @@
         own_arrived(p)
         when(jnp.logical_not(first))(lambda: y_copy(0, p).start())
         when(end, yc == 0, kc == 1)(lambda: far_copy(p).start())
+        when(end, yc == 0, kc == 1, p == steps - 2)(lambda: end_start(2))
 
     own_left.wait()
-    when(end, yc == 0, kc == 0)(lambda: each(lambda p: far_copy(p).start()))
+
+    @when(end, yc == 0, kc == 0)
+    def _():
+        each(lambda p: far_copy(p).start(), 0, steps - 1)
+        end_start(2)
+        far_copy(steps - 1).start()
+
     each(lambda p: y_copy(1, p).start())
-    when(end, yc == 0)(lambda: each(end_start, early))
+    when(end, yc == 0)(lambda: end_start(3))
 
     row = lax.broadcasted_iota(jnp.int32, (TILE, TILE), 0)
     column = lax.broadcasted_iota(jnp.int32, (TILE, TILE), 1)
@@ -509,12 +522,13 @@
     each(lambda q: turn(zc, q))
 
     def pass_on(q, h):
-        arrived(half_slot(3, q, h), end_recv.at[q, h])
-        mid_copy(q, h).start()
+        n, at = cut(q)
+        arrived(cut_slot(3, q, h, n), end_recv.at[at + h])
+        mid_copy(q, h, n).start()
 
     def end_arrived(q):
-        for h in range(2):
-            pass_on(q, h)
+        arrived(right_slot(3, q), end_recv.at[q])
+        mid_copy(q).start()
         turn(3, q)
 
     def share(p):
@@ -526,12 +540,13 @@
         arrived(y_slot(1 - yc, 0, p, k), y_recv.at[0, p])
         s_copy(0, p, 0).start()
         when(end, yc == 1)(lambda: far_copy(p).start())
+        when(end, yc == 1, p == steps - 2)(lambda: end_start(2))
         arrived(right_slot(zc - 1, p), in_recv.at[0, p])
         when(inner)(lambda: fwd_copy(p).start())
         turn(zc - 1, p)
         when(inner, p >= 1, p <= early)(lambda: end_arrived(p - 1))
 
-    when(end, yc == 1)(lambda: each(end_start, early))
+    when(end, yc == 1)(lambda: end_start(3))
     arrived(y_slot(1 - yc, 0, 0, 1 - k, steps), s_recv.at[0])
     late = 2 - yc
     groups = ((0, early), (early, early + 1), (early + 1, steps))
@@ -576,28 +591,30 @@
         share(2)
         far_turn(0)
         product_one(0, 0)
+        pass_on(2, 0)
+        pass_on(2, 1)
+        turn(3, 2)
+        product_one(3, 2)
+        y_arrived(1)
+        far_turn(1)
+        product_one(0, 1)
+        late_part(0)
         share(3)
         arrived(left_far.at[:, pl.ds(pl.multiple_of((1 - k) * half, half), half)], a_recv.at[0])
         far_product(0)
-        y_arrived(1)
+        y_arrived(2)
         far_send_on(0)
-        pass_on(2, 0)
-        far_turn(1)
+        pass_on(3, 0)
         far_product(1)
         far_send_on(1)
-        pass_on(2, 1)
-        product_one(0, 1)
-        turn(3, 2)
-        y_arrived(2)
-        product_one(3, 2)
-        pass_on(3, 0)
-        late_part(0)
-        late_part(1)
         pass_on(3, 1)
         far_turn(2)
         far_product(2)
+        pass_on(3, 2)
+        far_send_on(2)
+        pass_on(3, 3)
+        late_part(1)
         y_arrived(3)
-        far_send_on(2)
         turn(3, 3)
         product_one(3, 3)
         product_one(0, 2)
@@ -675,7 +692,7 @@
             pltpu.VMEM((left_dev * heads // 2, 2 * CH * CH), jnp.bfloat16),
             pltpu.VMEM((steps, left_dev * heads // 2, 2 * pair), jnp.bfloat16),
             pltpu.VMEM((steps, left_dev // 4, 4, heads, pair), jnp.float32),
-            dma((9,)), dma((2, steps)), dma((steps,)), dma((steps, 2)), dma((steps,)), dma((2, steps)), dma((4,)), dma((1,)), dma((4,)),
+            dma((9,)), dma((2, steps)), dma((steps,)), dma((8,)), dma((steps,)), dma((2, steps)), dma((4,)), dma((1,)), dma((4,)),
         ],
         compiler_params=pltpu.CompilerParams(collective_id=0, has_side_effects=True, vmem_limit_bytes=38000 * 1024),
         name="pair_mean",

time: 64.8 us -> 64.7 us (level)
  no operation moved by 1% of the time
where the time goes in v6:
time: 64.7 us; the launch traced here: 64.5 us
  Pallas kernels  63.5 us (98%)
  local copies, waits for them, and re-layouts  0.97 us (1%)
    pallas_call x1, Pallas kernels, folded_call(): pl.pallas_call(folded, out_shape=jax.ShapeDtypeStruct((left_dev, right_de...  63.5 us

profile of v6, /device:TPU:0, one launch (start us, length us, event | category | flops | bytes accessed | tf_op | source)
XLA Modules:
  0.0 64.5 jit_solution(3964160122396406555)
XLA Ops:
  0.0 63.5 %pair_mean.1 = f32[64,32,128]{2,1,0:T(8,128)S(1)} custom-call(bf16[512,2048]{1,0:T(8,128)(2,1)} %left_ref.1, bf16[512,1024]{1,0:T(8,128)(2,1)} %right_ref.1, s32[32,64]{1,0:T(8,128)} %bitcast.1, bf16[1024,128]{1,0:T(8,128)(2,1)} %w_hbm.1), custom_call_target="tpu_custom_call" | custom-call | tf_op jit(solution)/shard_map/pair_mean/pallas_call | solution.py:674
  63.6 1.0 %copy.6 = f32[64,32,128]{2,1,0:T(8,128)} copy(f32[64,32,128]{2,1,0:T(8,128)S(1)} %pair_mean.1) | data formatting | bytes 2097152

commit v7 on v6

--- a/solution.py
+++ b/solution.py
@@ -600,27 +600,27 @@
         product_one(0, 1)
         late_part(0)
         share(3)
+        pass_on(3, 0)
         arrived(left_far.at[:, pl.ds(pl.multiple_of((1 - k) * half, half), half)], a_recv.at[0])
         far_product(0)
         y_arrived(2)
+        pass_on(3, 1)
         far_send_on(0)
-        pass_on(3, 0)
         far_product(1)
+        pass_on(3, 2)
         far_send_on(1)
-        pass_on(3, 1)
+        pass_on(3, 3)
         far_turn(2)
         far_product(2)
-        pass_on(3, 2)
         far_send_on(2)
-        pass_on(3, 3)
         late_part(1)
         y_arrived(3)
         turn(3, 3)
         product_one(3, 3)
-        product_one(0, 2)
         far_turn(3)
         far_product(3)
         far_send_on(3)
+        product_one(0, 2)
         late_part(2)
         product_one(0, 3)
 

time: 64.7 us -> 63.1 us (0.975)
  Pallas kernels: 63.5 us -> 62 us
    pallas_call x1, Pallas kernels: 63.5 us -> 62 us  [folded_call(): pl.pallas_call(folded, out_shape=jax.ShapeDtypeStruct((left_dev, right_de...]
where the time goes in v7:
time: 63.1 us; the launch traced here: 62.9 us
  Pallas kernels  62 us (98%)
  local copies, waits for them, and re-layouts  0.97 us (2%)
    pallas_call x1, Pallas kernels, folded_call(): pl.pallas_call(folded, out_shape=jax.ShapeDtypeStruct((left_dev, right_de...  62 us

profile of v7, /device:TPU:0, one launch (start us, length us, event | category | flops | bytes accessed | tf_op | source)
XLA Modules:
  0.0 62.9 jit_solution(7101571465951913279)
XLA Ops:
  0.0 62.0 %pair_mean.1 = f32[64,32,128]{2,1,0:T(8,128)S(1)} custom-call(bf16[512,2048]{1,0:T(8,128)(2,1)} %left_ref.1, bf16[512,1024]{1,0:T(8,128)(2,1)} %right_ref.1, s32[32,64]{1,0:T(8,128)} %bitcast.1, bf16[1024,128]{1,0:T(8,128)(2,1)} %w_hbm.1), custom_call_target="tpu_custom_call" | custom-call | tf_op jit(solution)/shard_map/pair_mean/pallas_call | solution.py:674
  62.0 1.0 %copy.6 = f32[64,32,128]{2,1,0:T(8,128)} copy(f32[64,32,128]{2,1,0:T(8,128)S(1)} %pair_mean.1) | data formatting | bytes 2097152

commit v8 on v7

--- a/solution.py
+++ b/solution.py
@@ -420,19 +420,20 @@
 
         lax.fori_loop(first, last, step, 0)
 
-    @when(inner)
-    def _():
-        @each
-        def _(q):
-            in_copy(-1, q).start()
-            in_copy(1, q).start()
-
-
-    @when(end)
-    def _():
-        end_start(0)
-        end_start(1)
-
+    def z_start():
+        @when(inner)
+        def _():
+            @each
+            def _(q):
+                in_copy(-1, q).start()
+                in_copy(1, q).start()
+
+        @when(end)
+        def _():
+            end_start(0)
+            end_start(1)
+
+    when(k == 0)(z_start)
     first = kc == yc
     when(first)(lambda: each(lambda p: y_copy(0, p, True).start()))
     own_left = pltpu.make_async_copy(left_ref, left_full.at[pl.ds(pl.multiple_of(r * rows, rows), rows), :], own_sem.at[0])
@@ -440,6 +441,7 @@
     weights = pltpu.make_async_copy(w_hbm, w_in, own_sem.at[2])
     counts_copy = pltpu.make_async_copy(counts_ref, counts_in, own_sem.at[3])
     each(lambda p: own_copy(p).start())
+    when(k == 1)(z_start)
     for copy in (own_left, own, weights, counts_copy):
         copy.start()
 
@@ -510,13 +512,14 @@
     def spot(i):
         return slice(i // 2 * lines, (i // 2 + 1) * lines), slice(i % 2 * pair, (i % 2 + 1) * pair)
 
-    def settle(q, add):
+    def emit(q, i, value):
+        at = pl.ds(pl.multiple_of(q * heads, heads), heads)
+        out_ref[pl.ds(i, quads, stride=4), at, :] = value / cover[:, i, at, :]
+
+    def settle(q):
         for i in range(4):
             value = out_v[q, :, i]
-            if add:
-                value = value + part[(q, *spot(i))].astype(jnp.float32).reshape(value.shape)
-            at = pl.ds(pl.multiple_of(q * heads, heads), heads)
-            out_ref[pl.ds(i, quads, stride=4), at, :] = value / cover[:, i, at, :]
+            emit(q, i, value + part[(q, *spot(i))].astype(jnp.float32).reshape(value.shape))
 
     own.wait()
     each(lambda q: turn(zc, q))
@@ -601,16 +604,17 @@
         late_part(0)
         share(3)
         pass_on(3, 0)
+        far_turn(2)
+        product_one(0, 2)
+        pass_on(3, 1)
         arrived(left_far.at[:, pl.ds(pl.multiple_of((1 - k) * half, half), half)], a_recv.at[0])
         far_product(0)
         y_arrived(2)
-        pass_on(3, 1)
         far_send_on(0)
+        pass_on(3, 2)
         far_product(1)
-        pass_on(3, 2)
         far_send_on(1)
         pass_on(3, 3)
-        far_turn(2)
         far_product(2)
         far_send_on(2)
         late_part(1)
@@ -620,14 +624,14 @@
         far_turn(3)
         far_product(3)
         far_send_on(3)
-        product_one(0, 2)
         late_part(2)
         product_one(0, 3)
 
         @each
         def _(q):
-            finish(q)
-            settle(q, False)
+            value = project(acc, q * TILE)
+            for i in range(4):
+                emit(q, i, value[spot(i)].reshape(quads, heads, pair))
 
         sent(0)
         sent(1)
@@ -659,7 +663,7 @@
         @each
         def _(q):
             arrived(part.at[q], far_recv.at[q])
-            settle(q, True)
+            settle(q)
 
 
 def folded_call(left_act, right_act, counts, w_out):

time: 63.1 us -> 63.4 us (level)
  no operation moved by 1% of the time
where the time goes in v8:
time: 63.4 us; the launch traced here: 63.2 us
  Pallas kernels  62.3 us (98%)
  local copies, waits for them, and re-layouts  0.97 us (2%)
    pallas_call x1, Pallas kernels, folded_call(): pl.pallas_call(folded, out_shape=jax.ShapeDtypeStruct((left_dev, right_de...  62.3 us

profile of v8, /device:TPU:0, one launch (start us, length us, event | category | flops | bytes accessed | tf_op | source)
XLA Modules:
  0.0 63.2 jit_solution(9702097197359071808)
XLA Ops:
  0.0 62.3 %pair_mean.1 = f32[64,32,128]{2,1,0:T(8,128)S(1)} custom-call(bf16[512,2048]{1,0:T(8,128)(2,1)} %left_ref.1, bf16[512,1024]{1,0:T(8,128)(2,1)} %right_ref.1, s32[32,64]{1,0:T(8,128)} %bitcast.1, bf16[1024,128]{1,0:T(8,128)(2,1)} %w_hbm.1), custom_call_target="tpu_custom_call" | custom-call | tf_op jit(solution)/shard_map/pair_mean/pallas_call | solution.py:678
  62.3 1.0 %copy.6 = f32[64,32,128]{2,1,0:T(8,128)} copy(f32[64,32,128]{2,1,0:T(8,128)S(1)} %pair_mean.1) | data formatting | bytes 2097152

commit v9 on v8

--- a/solution.py
+++ b/solution.py
@@ -441,13 +441,13 @@
     weights = pltpu.make_async_copy(w_hbm, w_in, own_sem.at[2])
     counts_copy = pltpu.make_async_copy(counts_ref, counts_in, own_sem.at[3])
     each(lambda p: own_copy(p).start())
-    when(k == 1)(z_start)
     for copy in (own_left, own, weights, counts_copy):
         copy.start()
 
     @each
     def _(p):
         own_arrived(p)
+        when(k == 1, p == 0)(z_start)
         when(jnp.logical_not(first))(lambda: y_copy(0, p).start())
         when(end, yc == 0, kc == 1)(lambda: far_copy(p).start())
         when(end, yc == 0, kc == 1, p == steps - 2)(lambda: end_start(2))
@@ -613,8 +613,8 @@
         far_send_on(0)
         pass_on(3, 2)
         far_product(1)
+        pass_on(3, 3)
         far_send_on(1)
-        pass_on(3, 3)
         far_product(2)
         far_send_on(2)
         late_part(1)

time: 63.4 us -> 64.5 us (1.017)
  Pallas kernels: 62.3 us -> 63.4 us
    pallas_call x1, Pallas kernels: 62.3 us -> 63.4 us  [folded_call(): pl.pallas_call(folded, out_shape=jax.ShapeDtypeStruct((left_dev, right_de...]
where the time goes in v9:
time: 64.5 us; the launch traced here: 64.4 us
  Pallas kernels  63.4 us (98%)
  local copies, waits for them, and re-layouts  0.97 us (2%)
    pallas_call x1, Pallas kernels, folded_call(): pl.pallas_call(folded, out_shape=jax.ShapeDtypeStruct((left_dev, right_de...  63.4 us

profile of v9, /device:TPU:0, one launch (start us, length us, event | category | flops | bytes accessed | tf_op | source)
XLA Modules:
  0.0 64.4 jit_solution(15660817271682444205)
XLA Ops:
  0.0 63.4 %pair_mean.1 = f32[64,32,128]{2,1,0:T(8,128)S(1)} custom-call(bf16[512,2048]{1,0:T(8,128)(2,1)} %left_ref.1, bf16[512,1024]{1,0:T(8,128)(2,1)} %right_ref.1, s32[32,64]{1,0:T(8,128)} %bitcast.1, bf16[1024,128]{1,0:T(8,128)(2,1)} %w_hbm.1), custom_call_target="tpu_custom_call" | custom-call | tf_op jit(solution)/shard_map/pair_mean/pallas_call | solution.py:678
  63.4 1.0 %copy.6 = f32[64,32,128]{2,1,0:T(8,128)} copy(f32[64,32,128]{2,1,0:T(8,128)S(1)} %pair_mean.1) | data formatting | bytes 2097152

commit v10 on v9

--- a/solution.py
+++ b/solution.py
@@ -420,20 +420,18 @@
 
         lax.fori_loop(first, last, step, 0)
 
-    def z_start():
-        @when(inner)
-        def _():
-            @each
-            def _(q):
-                in_copy(-1, q).start()
-                in_copy(1, q).start()
-
-        @when(end)
-        def _():
-            end_start(0)
-            end_start(1)
-
-    when(k == 0)(z_start)
+    @when(inner)
+    def _():
+        @each
+        def _(q):
+            in_copy(-1, q).start()
+            in_copy(1, q).start()
+
+    @when(end)
+    def _():
+        end_start(0)
+        end_start(1)
+
     first = kc == yc
     when(first)(lambda: each(lambda p: y_copy(0, p, True).start()))
     own_left = pltpu.make_async_copy(left_ref, left_full.at[pl.ds(pl.multiple_of(r * rows, rows), rows), :], own_sem.at[0])
@@ -447,7 +445,6 @@
     @each
     def _(p):
         own_arrived(p)
-        when(k == 1, p == 0)(z_start)
         when(jnp.logical_not(first))(lambda: y_copy(0, p).start())
         when(end, yc == 0, kc == 1)(lambda: far_copy(p).start())
         when(end, yc == 0, kc == 1, p == steps - 2)(lambda: end_start(2))

time: 64.5 us -> 63.2 us (0.980)
  Pallas kernels: 63.4 us -> 62 us
    pallas_call x1, Pallas kernels: 63.4 us -> 62 us  [folded_call(): pl.pallas_call(folded, out_shape=jax.ShapeDtypeStruct((left_dev, right_de...]
where the time goes in v10:
time: 63.2 us; the launch traced here: 63 us
  Pallas kernels  62 us (98%)
  local copies, waits for them, and re-layouts  0.97 us (2%)
    pallas_call x1, Pallas kernels, folded_call(): pl.pallas_call(folded, out_shape=jax.ShapeDtypeStruct((left_dev, right_de...  62 us

profile of v10, /device:TPU:0, one launch (start us, length us, event | category | flops | bytes accessed | tf_op | source)
XLA Modules:
  0.0 63.0 jit_solution(12787967055403748720)
XLA Ops:
  0.0 62.0 %pair_mean.1 = f32[64,32,128]{2,1,0:T(8,128)S(1)} custom-call(bf16[512,2048]{1,0:T(8,128)(2,1)} %left_ref.1, bf16[512,1024]{1,0:T(8,128)(2,1)} %right_ref.1, s32[32,64]{1,0:T(8,128)} %bitcast.1, bf16[1024,128]{1,0:T(8,128)(2,1)} %w_hbm.1), custom_call_target="tpu_custom_call" | custom-call | tf_op jit(solution)/shard_map/pair_mean/pallas_call | solution.py:675
  62.1 1.0 %copy.6 = f32[64,32,128]{2,1,0:T(8,128)} copy(f32[64,32,128]{2,1,0:T(8,128)S(1)} %pair_mean.1) | data formatting | bytes 2097152

commit v11 on v10

--- a/solution.py
+++ b/solution.py
@@ -570,7 +570,11 @@
 
     def far_send_on(q):
         part[q] = project(acc_far, 0).astype(part.dtype)
-        part_copy(q).start()
+        pl.when(k == 0)(lambda: part_copy(q).start())
+        if q >= 1:
+            pl.when(k == 1)(lambda: part_copy(q - 1).start())
+        if q == steps - 1:
+            pl.when(k == 1)(lambda: part_copy(q).start())
 
     def finish(q):
         value = project(acc, q * TILE)

time: 63.2 us -> 64.4 us (1.019)
  Pallas kernels: 62 us -> 63.3 us
    pallas_call x1, Pallas kernels: 62 us -> 63.3 us  [folded_call(): pl.pallas_call(folded, out_shape=jax.ShapeDtypeStruct((left_dev, right_de...]
where the time goes in v11:
time: 64.4 us; the launch traced here: 64.3 us
  Pallas kernels  63.3 us (98%)
  local copies, waits for them, and re-layouts  0.97 us (2%)
    pallas_call x1, Pallas kernels, folded_call(): pl.pallas_call(folded, out_shape=jax.ShapeDtypeStruct((left_dev, right_de...  63.3 us

profile of v11, /device:TPU:0, one launch (start us, length us, event | category | flops | bytes accessed | tf_op | source)
XLA Modules:
  0.0 64.3 jit_solution(5067786473549259458)
XLA Ops:
  0.0 63.3 %pair_mean.1 = f32[64,32,128]{2,1,0:T(8,128)S(1)} custom-call(bf16[512,2048]{1,0:T(8,128)(2,1)} %left_ref.1, bf16[512,1024]{1,0:T(8,128)(2,1)} %right_ref.1, s32[32,64]{1,0:T(8,128)} %bitcast.1, bf16[1024,128]{1,0:T(8,128)(2,1)} %w_hbm.1), custom_call_target="tpu_custom_call" | custom-call | tf_op jit(solution)/shard_map/pair_mean/pallas_call | solution.py:679
  63.3 1.0 %copy.6 = f32[64,32,128]{2,1,0:T(8,128)} copy(f32[64,32,128]{2,1,0:T(8,128)S(1)} %pair_mean.1) | data formatting | bytes 2097152

commit v12 on v10

--- a/solution.py
+++ b/solution.py
@@ -601,23 +601,23 @@
         late_part(0)
         share(3)
         pass_on(3, 0)
-        far_turn(2)
-        product_one(0, 2)
-        pass_on(3, 1)
         arrived(left_far.at[:, pl.ds(pl.multiple_of((1 - k) * half, half), half)], a_recv.at[0])
         far_product(0)
         y_arrived(2)
+        pass_on(3, 1)
         far_send_on(0)
+        far_product(1)
         pass_on(3, 2)
-        far_product(1)
+        far_send_on(1)
         pass_on(3, 3)
-        far_send_on(1)
+        far_turn(2)
         far_product(2)
         far_send_on(2)
         late_part(1)
         y_arrived(3)
         turn(3, 3)
         product_one(3, 3)
+        product_one(0, 2)
         far_turn(3)
         far_product(3)
         far_send_on(3)

time: 63.2 us -> 63.1 us (level)
  no operation moved by 1% of the time
where the time goes in v12:
time: 63.1 us; the launch traced here: 62.9 us
  Pallas kernels  62 us (98%)
  local copies, waits for them, and re-layouts  0.97 us (2%)
    pallas_call x1, Pallas kernels, folded_call(): pl.pallas_call(folded, out_shape=jax.ShapeDtypeStruct((left_dev, right_de...  62 us

profile of v12, /device:TPU:0, one launch (start us, length us, event | category | flops | bytes accessed | tf_op | source)
XLA Modules:
  0.0 62.9 jit_solution(3378003906461185270)
XLA Ops:
  0.0 62.0 %pair_mean.1 = f32[64,32,128]{2,1,0:T(8,128)S(1)} custom-call(bf16[512,2048]{1,0:T(8,128)(2,1)} %left_ref.1, bf16[512,1024]{1,0:T(8,128)(2,1)} %right_ref.1, s32[32,64]{1,0:T(8,128)} %bitcast.1, bf16[1024,128]{1,0:T(8,128)(2,1)} %w_hbm.1), custom_call_target="tpu_custom_call" | custom-call | tf_op jit(solution)/shard_map/pair_mean/pallas_call | solution.py:675
  62.0 1.0 %copy.6 = f32[64,32,128]{2,1,0:T(8,128)} copy(f32[64,32,128]{2,1,0:T(8,128)S(1)} %pair_mean.1) | data formatting | bytes 2097152

commit v13 on v12

--- a/solution.py
+++ b/solution.py
@@ -424,8 +424,8 @@
     def _():
         @each
         def _(q):
+            in_copy(1, q).start()
             in_copy(-1, q).start()
-            in_copy(1, q).start()
 
     @when(end)
     def _():
@@ -617,10 +617,10 @@
         y_arrived(3)
         turn(3, 3)
         product_one(3, 3)
-        product_one(0, 2)
         far_turn(3)
         far_product(3)
         far_send_on(3)
+        product_one(0, 2)
         late_part(2)
         product_one(0, 3)
 

time: 63.1 us -> 63.1 us (level)
  no operation moved by 1% of the time
where the time goes in v13:
time: 63.1 us; the launch traced here: 62.9 us
  Pallas kernels  62 us (98%)
  local copies, waits for them, and re-layouts  0.97 us (2%)
    pallas_call x1, Pallas kernels, folded_call(): pl.pallas_call(folded, out_shape=jax.ShapeDtypeStruct((left_dev, right_de...  62 us

profile of v13, /device:TPU:0, one launch (start us, length us, event | category | flops | bytes accessed | tf_op | source)
XLA Modules:
  0.0 62.9 jit_solution(446230471221034454)
XLA Ops:
  0.0 62.0 %pair_mean.1 = f32[64,32,128]{2,1,0:T(8,128)S(1)} custom-call(bf16[512,2048]{1,0:T(8,128)(2,1)} %left_ref.1, bf16[512,1024]{1,0:T(8,128)(2,1)} %right_ref.1, s32[32,64]{1,0:T(8,128)} %bitcast.1, bf16[1024,128]{1,0:T(8,128)(2,1)} %w_hbm.1), custom_call_target="tpu_custom_call" | custom-call | tf_op jit(solution)/shard_map/pair_mean/pallas_call | solution.py:675
  62.0 1.0 %copy.6 = f32[64,32,128]{2,1,0:T(8,128)} copy(f32[64,32,128]{2,1,0:T(8,128)S(1)} %pair_mean.1) | data formatting | bytes 2097152

commit v14 on v13

--- a/solution.py
+++ b/solution.py
@@ -608,8 +608,8 @@
         far_send_on(0)
         far_product(1)
         pass_on(3, 2)
+        pass_on(3, 3)
         far_send_on(1)
-        pass_on(3, 3)
         far_turn(2)
         far_product(2)
         far_send_on(2)

time: 63.1 us -> 63.1 us (level)
  no operation moved by 1% of the time
where the time goes in v14:
time: 63.1 us; the launch traced here: 62.9 us
  Pallas kernels  62 us (98%)
  local copies, waits for them, and re-layouts  0.97 us (2%)
    pallas_call x1, Pallas kernels, folded_call(): pl.pallas_call(folded, out_shape=jax.ShapeDtypeStruct((left_dev, right_de...  62 us

profile of v14, /device:TPU:0, one launch (start us, length us, event | category | flops | bytes accessed | tf_op | source)
XLA Modules:
  0.0 62.9 jit_solution(9113113684430961933)
XLA Ops:
  0.0 62.0 %pair_mean.1 = f32[64,32,128]{2,1,0:T(8,128)S(1)} custom-call(bf16[512,2048]{1,0:T(8,128)(2,1)} %left_ref.1, bf16[512,1024]{1,0:T(8,128)(2,1)} %right_ref.1, s32[32,64]{1,0:T(8,128)} %bitcast.1, bf16[1024,128]{1,0:T(8,128)(2,1)} %w_hbm.1), custom_call_target="tpu_custom_call" | custom-call | tf_op jit(solution)/shard_map/pair_mean/pallas_call | solution.py:675
  62.0 1.0 %copy.6 = f32[64,32,128]{2,1,0:T(8,128)} copy(f32[64,32,128]{2,1,0:T(8,128)S(1)} %pair_mean.1) | data formatting | bytes 2097152
